TPU v7x, 32 devices: a whole 2x2x4 slice. The times are simulated.
32 devices in a mesh: group: 2 (over x), mem: 16 (over z, y, core).
Axes of the slice: x: 2, y: 2, z: 4, core: 2. Of those that a mesh axis runs over, the one named last changes fastest.
Arguments:
- perturbations: bfloat16 [32, 256, 4, 1, 256], P(('group', 'mem')), parts along dimension 0, may hold values from -6 to 6
- gradient: bfloat16 [512, 4, 1, 256], P(('group', 'mem')), parts along dimension 0, may hold values from -6 to 6
Outputs:
- increment: bfloat16 [512, 4, 1, 256], P(('group', 'mem')), parts along dimension 0
There are 2 independent parts, one for each index of `group`. A program takes and returns all parts, laid end to end along the dimension named above; each array names one. Nothing has to cross between parts.
All inputs are finite; a program needn't handle non-finite values.
Results may differ from a plain program's by a relative error of at most 0.0085.
Values may be sent and summed in bfloat16 or wider, within the bound.
No kernel may reach another device: no remote copies, remote signals or barrier semaphores. Data moves between devices by JAX's collectives and lax.ppermute only.
A program may use at most 64 MiB of HBM per device.

v0:
```python
import jax
import jax.numpy as jnp
from jax import lax
from jax.sharding import PartitionSpec as P

REACH = 8


def make_band(order):
    rows = jnp.arange(order, dtype=jnp.int32)
    offset = (rows[:, None] - rows[None, :]).astype(jnp.float32)
    weights = jnp.exp(-(offset * offset) / (4.0 * REACH))
    inside = jnp.abs(offset) <= REACH
    return jnp.where(inside, weights, jnp.float32(0.0)).astype(jnp.bfloat16)


def per_device(perturbations, gradient):
    local_rows, nvars, levels, columns = gradient.shape
    count_here = perturbations.shape[0]
    grid_rows = perturbations.shape[1]
    members = count_here * lax.axis_size("mem")
    band_x = make_band(columns)
    band_y = make_band(grid_rows)
    row_block = lax.all_to_all(perturbations, "mem", split_axis=1, concat_axis=0, tiled=True)
    mixed = jnp.sum(
        row_block.astype(jnp.float32) * gradient.astype(jnp.float32)[None], axis=2
    ).astype(jnp.bfloat16)
    along_x = jnp.dot(
        mixed.reshape(members * local_rows * levels, columns),
        band_x,
        preferred_element_type=jnp.float32,
    )
    along_x = along_x.astype(jnp.bfloat16).reshape(members, local_rows, levels, columns)
    whole_field = lax.all_to_all(along_x, "mem", split_axis=0, concat_axis=1, tiled=True)
    filtered = jnp.dot(
        band_y,
        whole_field.reshape(count_here, grid_rows, levels * columns)[0],
        preferred_element_type=jnp.float32,
    )
    filtered = filtered.astype(jnp.bfloat16).reshape(count_here, grid_rows, levels, columns)
    row_field = lax.all_to_all(filtered, "mem", split_axis=1, concat_axis=0, tiled=True)
    total = jnp.sum(
        row_block.astype(jnp.float32) * row_field.astype(jnp.float32)[:, :, None], axis=0
    )
    return (total * (1.0 / (members - 1))).astype(jnp.bfloat16)


def solution(mesh):
    in_specs = (P(("group", "mem"), None, None, None, None), P(("group", "mem"), None, None, None))
    out_specs = P(("group", "mem"), None, None, None)
    return jax.shard_map(
        per_device, mesh=mesh, in_specs=in_specs, out_specs=out_specs, check_vma=False
    )
```

profile of v0, /device:TPU:0, one launch (start us, length us, event | category | flops | bytes accessed | tf_op | source)
XLA Modules:
  0.0 49.0 jit_solution(8863171677678697585)
XLA Ops:
  0.0 0.0 copy-start
  0.0 7.5 %all-to-all-start = ((bf16[1,256,4,1,256]{4,2,3,0,1:T(4,128)(2,1)}), bf16[1,256,4,1,256]{4,2,3,0,1:T(4,128)(2,1)S(1)}, u32[]{:S(2)}, u32[]{:S(2)}) async-start(bf16[1,256,4,1,256]{4,2,3,0,1:T(4,128)(2,1)} %bitcast.27), calls=%async_computation | async-start | bytes 1048576 | tf_op jit(solution)/shard_map/all_to_all | solution.py:24
  7.6 0.0 copy-done
  7.6 14.2 %all-to-all-done = bf16[1,256,4,1,256]{4,2,3,0,1:T(4,128)(2,1)S(1)} async-done(((bf16[1,256,4,1,256]{4,2,3,0,1:T(4,128)(2,1)}), bf16[1,256,4,1,256]{4,2,3,0,1:T(4,128)(2,1)S(1)}, u32[]{:S(2)}, u32[]{:S(2)}) %all-to-all-start) | async-done | bytes 524320 | tf_op jit(solution)/shard_map/all_to_all | solution.py:24
  21.8 0.2 mul.62
  22.0 0.9 %multiply_reduce_fusion.1 = bf16[256,256]{1,0:T(8,128)(2,1)S(1)} fusion(f32[1,256,4,1,256]{4,2,3,0,1:T(4,128)S(1)} %bitcast.23, bf16[1,256,4,1,256]{4,2,3,0,1:T(4,128)(2,1)S(1)} %all-to-all-done), kind=kLoop, calls=%fused_computation.4 | loop fusion | flops 720896 | bytes 1703936 | tf_op jit(solution)/shard_map/reduce_sum | solution.py:25
  22.9 0.2 convolution_convert_fusion.1
  23.1 11.9 %all_to_all.12 = bf16[16,16,1,256]{3,1,2,0:T(8,128)(2,1)S(1)} all-to-all(bf16[16,16,1,256]{3,1,2,0:T(8,128)(2,1)S(1)} %bitcast.28), channel_id=1, replica_groups=mesh['group'=2,'mem'=16] {'mem'}, dimensions={0} | all-to-all | bytes 262144 | tf_op jit(solution)/shard_map/all_to_all | solution.py:34
  35.0 0.2 fusion
  35.2 0.2 copy.8
  35.4 0.5 %broadcast.44 = bf16[]{:T(256)} broadcast(bf16[]{:T(256)} %constant.20), dimensions={} | broadcast | bytes 4
  35.9 1.4 %reduce.3 = bf16[256,256]{1,0:T(8,128)(2,1)S(1)} reduce(bf16[256,1,1,256]{3,2,1,0:T(2,128)(2,1)S(1)} %bitcast.24, bf16[]{:T(256)} %broadcast.44), dimensions={1,2}, to_apply=%bitcast.21.reduce_sub_computation | reduce | bytes 262146
  37.4 10.5 %all_to_all.13 = bf16[16,2,2048]{2,1,0:T(2,128)(2,1)S(1)} all-to-all(bf16[16,2,2048]{2,1,0:T(2,128)(2,1)S(1)} %reshape.90), channel_id=1, replica_groups=mesh['group'=2,'mem'=16] {'mem'}, dimensions={0} | all-to-all | bytes 262144 | tf_op jit(solution)/shard_map/all_to_all | solution.py:41
  47.9 0.1 reshape.91
  48.0 0.3 multiply_reduce_fusion
  48.3 0.6 %fusion.2 = bf16[16,4,1,256]{3,1,2,0:T(4,128)(2,1)} fusion(f32[16,4,256]{2,1,0:T(4,128)S(1)} %multiply_reduce_fusion), kind=kLoop, calls=%fused_computation.9 | loop fusion | flops 32768 | bytes 98304 | tf_op jit(solution)/shard_map/convert_element_type | solution.py:45
  (3 shorter events, 0.1 us)
Async XLA Ops:
  0.0 7.6 %copy-start = (bf16[16,4,1,256]{3,1,2,0:T(4,128)(2,1)S(1)}, bf16[16,4,1,256]{3,1,2,0:T(4,128)(2,1)}, u32[]{:S(2)}) copy-start(bf16[16,4,1,256]{3,1,2,0:T(4,128)(2,1)} %param.3) | copy-start | bytes 98308
  0.0 21.8 %all-to-all-start = ((bf16[1,256,4,1,256]{4,2,3,0,1:T(4,128)(2,1)}), bf16[1,256,4,1,256]{4,2,3,0,1:T(4,128)(2,1)S(1)}, u32[]{:S(2)}, u32[]{:S(2)}) async-start(bf16[1,256,4,1,256]{4,2,3,0,1:T(4,128)(2,1)} %bitcast.27), calls=%async_computation | async-start | bytes 1048576 | tf_op jit(solution)/shard_map/all_to_all | solution.py:24
where the time goes:
time: 49.3 us; the launch traced here: 49 us
  blocking collectives  22.4 us (45%)
  waiting for transfers between devices  14.2 us (29%)
  starting transfers between devices  7.55 us (15%)
  other arithmetic  3.2 us (6%)
  local copies, waits for them, and re-layouts  1.09 us (2%)
    all_to_all x1, waiting for transfers between devices, per_device(): lax.all_to_all(perturbations, 'mem', split_axis=1, concat_axis=0, tiled=T...  14.2 us
    all_to_all x1, blocking collectives, per_device(): lax.all_to_all(along_x, 'mem', split_axis=0, concat_axis=1, tiled=True)  11.9 us
    all_to_all x1, blocking collectives, per_device(): lax.all_to_all(filtered, 'mem', split_axis=1, concat_axis=0, tiled=True)  10.5 us
    all_to_all x1, starting transfers between devices, per_device(): lax.all_to_all(perturbations, 'mem', split_axis=1, concat_axis=0, tiled=T...  7.55 us
    unnamed x1, other arithmetic  1.41 us
  transfers between devices with their start and end apart: 1, of which 1 were waited for; matrix products, arithmetic and copies ran while one was open for 0% of the time, Pallas kernels for 0%

commit v1 on v0

--- a/solution.py
+++ b/solution.py
@@ -1,9 +1,16 @@
+import functools
+
 import jax
 import jax.numpy as jnp
 from jax import lax
+from jax.experimental import pallas as pl
+from jax.experimental.pallas import tpu as pltpu
 from jax.sharding import PartitionSpec as P
 
+
 REACH = 8
+GRANT = 16 << 20
+FIRST_GRANT = 16 << 20
 
 
 def make_band(order):
@@ -14,8 +21,8 @@
     return jnp.where(inside, weights, jnp.float32(0.0)).astype(jnp.bfloat16)
 
 
-def per_device(perturbations, gradient):
-    local_rows, nvars, levels, columns = gradient.shape
+def by_rows(perturbations, gradient):
+    local_rows, _, levels, columns = gradient.shape
     count_here = perturbations.shape[0]
     grid_rows = perturbations.shape[1]
     members = count_here * lax.axis_size("mem")
@@ -32,10 +39,9 @@
     )
     along_x = along_x.astype(jnp.bfloat16).reshape(members, local_rows, levels, columns)
     whole_field = lax.all_to_all(along_x, "mem", split_axis=0, concat_axis=1, tiled=True)
-    filtered = jnp.dot(
-        band_y,
-        whole_field.reshape(count_here, grid_rows, levels * columns)[0],
-        preferred_element_type=jnp.float32,
+    whole_field = whole_field.reshape(count_here, grid_rows, levels * columns)
+    filtered = jnp.stack(
+        [jnp.dot(band_y, field, preferred_element_type=jnp.float32) for field in whole_field]
     )
     filtered = filtered.astype(jnp.bfloat16).reshape(count_here, grid_rows, levels, columns)
     row_field = lax.all_to_all(filtered, "mem", split_axis=1, concat_axis=0, tiled=True)
@@ -45,9 +51,178 @@
     return (total * (1.0 / (members - 1))).astype(jnp.bfloat16)
 
 
+HALF, PAIR, SIDE, CORE = 8, 4, 2, 1
+PEERS = (PAIR + SIDE, SIDE, PAIR)
+
+
+def swap(array, bits):
+    return lax.ppermute(array, "mem", [(i, i ^ bits) for i in range(16)])
+
+
+def edges(array):
+    pairs = []
+    for i in range(16):
+        half, place, core = i // 8, i // 2 % 4, i % 2
+        place = (place + (1 if core else 3)) % 4
+        pairs.append((i, half * 8 + place * 2 + core))
+    return lax.ppermute(array, "mem", pairs)
+
+
+def first_row(strip, chip, rows):
+    start = jnp.clip(chip * strip - REACH, 0, rows - strip - 2 * REACH)
+    return start, chip * strip - start
+
+
+def window_kernel(strip, wanted, me_ref, member_ref, *refs):
+    outs, sem = refs[:-1], refs[-1]
+    me = me_ref[0]
+    rows = member_ref.shape[0]
+    copies = []
+    for bits, out in zip(wanted, outs):
+        start, _ = first_row(strip, (me ^ bits) // 2, rows)
+        copies.append(pltpu.make_async_copy(member_ref.at[pl.ds(start, strip + 2 * REACH)], out, sem.at[len(copies)]))
+    for copy in copies:
+        copy.start()
+    for copy in copies:
+        copy.wait()
+
+
+def windows(me, member, strip, wanted, grant):
+    _, nvars, columns = member.shape
+    shape = (strip + 2 * REACH, nvars, columns)
+    count = len(wanted)
+    return pl.pallas_call(
+        functools.partial(window_kernel, strip, wanted),
+        out_shape=[jax.ShapeDtypeStruct(shape, member.dtype)] * count,
+        in_specs=[pl.BlockSpec(memory_space=pltpu.SMEM), pl.BlockSpec(memory_space=pltpu.HBM)],
+        out_specs=[pl.BlockSpec(memory_space=pltpu.VMEM)] * count,
+        scratch_shapes=[pltpu.SemaphoreType.DMA((count,))],
+        compiler_params=pltpu.CompilerParams(vmem_limit_bytes=grant),
+    )(me, member)
+
+
+def strip_kernel(rows, far, me_ref, a_ref, b_ref, c_ref, d_ref, block_ref, mate_ref, edge_ref, edge_mate_ref, band_ref,
+                 own_ref, other_ref, grad_ref, mixed_ref, total_ref):
+    me = me_ref[0]
+    core, place = me % 2, me // 2 % 4
+    part, reach = block_ref.shape[0], edge_ref.shape[1]
+    strip = 2 * part
+    chips = rows // strip
+    chip = (me ^ (HALF * far)) // 2
+    _, at = first_row(strip, chip, rows)
+    span = strip + 2 * reach
+
+    grad_ref[...] = jnp.zeros_like(grad_ref)
+    grad_ref[pl.ds(at + core * part, part)] = block_ref[...]
+    grad_ref[pl.ds(at + (1 - core) * part, part)] = mate_ref[...]
+    before = jnp.where(place == 0, 1 - far, far)
+    after = jnp.where(place == 3, 1 - far, far)
+
+    @pl.when(jnp.logical_and(chip > 0, core == 0))
+    def _():
+        grad_ref[pl.ds(at - reach, reach)] = edge_mate_ref[before]
+
+    @pl.when(jnp.logical_and(chip > 0, core == 1))
+    def _():
+        grad_ref[pl.ds(at - reach, reach)] = edge_ref[before]
+
+    @pl.when(jnp.logical_and(chip < chips - 1, core == 0))
+    def _():
+        grad_ref[pl.ds(at + strip, reach)] = edge_ref[after]
+
+    @pl.when(jnp.logical_and(chip < chips - 1, core == 1))
+    def _():
+        grad_ref[pl.ds(at + strip, reach)] = edge_mate_ref[after]
+
+    grad = grad_ref[...].astype(jnp.float32)
+    members = (a_ref, b_ref, c_ref, d_ref)
+    for k, ref in enumerate(members):
+        mixed = jnp.sum(ref[...].astype(jnp.float32) * grad, axis=1)
+        mixed_ref[pl.ds(k * span, span)] = mixed.astype(jnp.bfloat16)
+    along = jnp.dot(mixed_ref[...], band_ref[...], preferred_element_type=jnp.float32).astype(jnp.bfloat16)
+    offset = lax.broadcasted_iota(jnp.int32, (strip, span), 0) + at - lax.broadcasted_iota(jnp.int32, (strip, span), 1)
+    wide = offset.astype(jnp.float32)
+    band = jnp.exp(-(wide * wide) / (4.0 * REACH))
+    band = jnp.where(jnp.abs(wide) <= REACH, band, 0.0).astype(jnp.bfloat16)
+    total = None
+    for k, ref in enumerate(members):
+        field = jnp.dot(band, along[k * span : (k + 1) * span], preferred_element_type=jnp.float32)
+        field = field.astype(jnp.bfloat16).astype(jnp.float32)
+        term = ref[pl.ds(at, strip)].astype(jnp.float32) * field[:, None, :]
+        total = term if total is None else total + term
+    total_ref[...] = total
+    own_ref[...] = total_ref[pl.ds(core * part, part)].astype(own_ref.dtype)
+    other_ref[...] = total_ref[pl.ds((1 - core) * part, part)].astype(other_ref.dtype)
+
+
+def one_strip(me, members, block, mate, edge, edge_mate, band, rows, far):
+    span, nvars, columns = members[0].shape
+    part = block.shape[0]
+    piece = (part, nvars, columns)
+    vmem = pl.BlockSpec(memory_space=pltpu.VMEM)
+    return pl.pallas_call(
+        functools.partial(strip_kernel, rows, far),
+        out_shape=[
+            jax.ShapeDtypeStruct(piece, jnp.bfloat16 if far else jnp.float32),
+            jax.ShapeDtypeStruct(piece, jnp.bfloat16),
+        ],
+        in_specs=[pl.BlockSpec(memory_space=pltpu.SMEM)] + [vmem] * 9,
+        out_specs=[vmem] * 2,
+        scratch_shapes=[
+            pltpu.VMEM((span, nvars, columns), jnp.bfloat16),
+            pltpu.VMEM((4 * span, columns), jnp.bfloat16),
+            pltpu.VMEM((2 * part, nvars, columns), jnp.float32),
+        ],
+        compiler_params=pltpu.CompilerParams(vmem_limit_bytes=GRANT),
+        name="far" if far else "near",
+    )(me, *members, block, mate, edge, edge_mate, band)
+
+
+def by_halves(perturbations, gradient):
+    local_rows, nvars, _, columns = gradient.shape
+    grid_rows = perturbations.shape[1]
+    strip = 2 * local_rows
+    members = lax.axis_size("mem")
+    at = lax.axis_index("mem")
+    me = at.reshape(1).astype(jnp.int32)
+    here = gradient.reshape(local_rows, nvars, columns)
+    member = perturbations.reshape(-1, nvars, columns)
+
+    far_out = windows(me, member, strip, [p ^ HALF for p in PEERS], FIRST_GRANT)
+    far_in = [swap(block, p) for block, p in zip(far_out, PEERS)]
+    there = swap(here, HALF)
+    *near_out, near_mine, far_mine = windows(me, member, strip, list(PEERS) + [0, HALF], GRANT)
+    near_in = [swap(block, p) for block, p in zip(near_out, PEERS)]
+    here_mate = swap(here, CORE)
+    both = jnp.stack([here, there])
+    both = jnp.where(at & 1 == 0, both[:, :REACH], both[:, -REACH:])
+    edge = edges(both)
+    there_mate = swap(there, CORE)
+    edge_mate = swap(edge, CORE)
+
+    band = make_band(columns)
+    args = (edge, edge_mate, band, grid_rows)
+    far_own, far_other = one_strip(me, [far_mine] + far_in, there, there_mate, *args, 1)
+    far_own, far_other = swap(far_own, HALF), swap(far_other, HALF + CORE)
+    near_own, near_other = one_strip(me, [near_mine] + near_in, here, here_mate, *args, 0)
+    near_other = swap(near_other, CORE)
+    total = near_own + near_other.astype(jnp.float32) + far_own.astype(jnp.float32) + far_other.astype(jnp.float32)
+    return (total * (1.0 / (members - 1))).astype(jnp.bfloat16).reshape(gradient.shape)
+
+
 def solution(mesh):
     in_specs = (P(("group", "mem"), None, None, None, None), P(("group", "mem"), None, None, None))
     out_specs = P(("group", "mem"), None, None, None)
+    halves = mesh.shape["mem"] == 16
+
+    def per_device(perturbations, gradient):
+        count_here, grid_rows, _, levels, _ = perturbations.shape
+        local_rows = gradient.shape[0]
+        if not halves:
+            return by_rows(perturbations, gradient)
+        assert count_here == 1 and levels == 1 and local_rows % 8 == 0 and grid_rows == 16 * local_rows
+        return by_halves(perturbations, gradient)
+
     return jax.shard_map(
         per_device, mesh=mesh, in_specs=in_specs, out_specs=out_specs, check_vma=False
     )

time: 49.3 us -> 33.7 us (0.68)
  blocking collectives: 22.4 us -> 0 us
  starting transfers between devices: 7.55 us -> 15.5 us
  Pallas kernels: 0 us -> 2.89 us
  waiting for transfers between devices: 14.2 us -> 12.4 us
  other arithmetic: 3.2 us -> 1.59 us
    all_to_all x2 -> x0, blocking collectives: 22.4 us -> none  [the longest x1 11.9 us: per_device(): lax.all_to_all(along_x, 'mem', split_axis=0, concat_axis=1, tiled=True)]
    ppermute x0 -> x14, starting transfers between devices: none -> 15.5 us  [the longest x13 14.1 us: swap(): return lax.ppermute(array, 'mem', [(i, i ^ bits) for i in range(16)])]
    all_to_all x1 -> x0, waiting for transfers between devices: 14.2 us -> none  [per_device(): lax.all_to_all(perturbations, 'mem', split_axis=1, concat_axis=0, tiled=T...]
    ppermute x0 -> x14, waiting for transfers between devices: none -> 12.4 us  [the longest x13 9.49 us: swap(): return lax.ppermute(array, 'mem', [(i, i ^ bits) for i in range(16)])]
    all_to_all x1 -> x0, starting transfers between devices: 7.55 us -> none  [per_device(): lax.all_to_all(perturbations, 'mem', split_axis=1, concat_axis=0, tiled=T...]
    pallas_call x0 -> x4, Pallas kernels: none -> 2.89 us  [the longest x2 1.85 us: one_strip(): pl.pallas_call(functools.partial(strip_kernel, rows, far), out_shape=[jax...]
    unnamed x1 -> x0, other arithmetic: 1.41 us -> none
    reduce_sum x2 -> x0, other arithmetic: 1.15 us -> none  [the longest x1 0.86 us: per_device(): jnp.sum(row_block.astype(jnp.float32) * gradient.astype(jnp.float32)[None...]
  transfers between devices with their start and end apart: 1 -> 14, of which waited for: 1 -> 7; matrix products, arithmetic and copies ran while one was open for 0% -> 3% of each run, Pallas kernels for 0% -> 9%
where the time goes in v1:
time: 33.7 us; the launch traced here: 33.5 us
  starting transfers between devices  15.5 us (46%)
  waiting for transfers between devices  12.4 us (37%)
  Pallas kernels  2.89 us (9%)
  other arithmetic  1.59 us (5%)
  local copies, waits for them, and re-layouts  1.05 us (3%)
    ppermute x13, starting transfers between devices, swap(): return lax.ppermute(array, 'mem', [(i, i ^ bits) for i in range(16)])  14.1 us
    ppermute x13, waiting for transfers between devices, swap(): return lax.ppermute(array, 'mem', [(i, i ^ bits) for i in range(16)])  9.49 us
    ppermute x1, waiting for transfers between devices, edges(): return lax.ppermute(array, 'mem', pairs)  2.92 us
    pallas_call x2, Pallas kernels, one_strip(): pl.pallas_call(functools.partial(strip_kernel, rows, far), out_shape=[jax...  1.85 us
    ppermute x1, starting transfers between devices, edges(): return lax.ppermute(array, 'mem', pairs)  1.46 us
    unnamed x6, local copies, waits for them, and re-layouts  1.05 us
    pallas_call x2, Pallas kernels, windows(): pl.pallas_call(functools.partial(window_kernel, strip, wanted), out_shape...  1.05 us
    select_n x1, other arithmetic, by_halves(): both = jnp.where(at & 1 == 0, both[:, :REACH], both[:, -REACH:])  0.83 us
  transfers between devices with their start and end apart: 14, of which 7 were waited for; matrix products, arithmetic and copies ran while one was open for 3% of the time, Pallas kernels for 9%

profile of v1, /device:TPU:0, one launch (start us, length us, event | category | flops | bytes accessed | tf_op | source)
XLA Modules:
  0.0 33.5 jit_solution(10052635478740487080)
XLA Ops:
  0.0 4.1 %collective-permute-start.4 = (bf16[16,4,256]{2,1,0:T(4,128)(2,1)}, bf16[16,4,256]{2,1,0:T(4,128)(2,1)S(1)}, u32[]{:S(2)}, u32[]{:S(2)}) collective-permute-start(bf16[16,4,256]{2,1,0:T(4,128)(2,1)} %bitcast.11), channel_id=1, source_target_pairs={{0,8},{1,9},{2,10},{3,11},{4,12},{5,13},{6,14},{7,15},{8,0},{9,1},... | collective-permute-start | bytes 98312 | tf_op jit(solution)/shard_map/ppermute | solution.py:59
  4.1 1.0 %copy-done = bf16[1,256,4,1,256]{4,2,3,1,0:T(4,128)(2,1)S(1)} copy-done((bf16[1,256,4,1,256]{4,2,3,1,0:T(4,128)(2,1)S(1)}, bf16[1,256,4,1,256]{4,2,3,1,0:T(4,128)(2,1)}, u32[]{:S(2)}) %copy-start) | copy-done | bytes 524312
  5.1 0.7 %shard_map.28 = (bf16[48,4,256]{2,1,0:T(4,128)(2,1)S(1)}, bf16[48,4,256]{2,1,0:T(4,128)(2,1)S(1)}, bf16[48,4,256]{2,1,0:T(4,128)(2,1)S(1)}, bf16[48,4,256]{2,1,0:T(4,128)(2,1)S(1)}, bf16[48,4,256]{2,1,0:T(4,128)(2,1)S(1)}) custom-call(s32[1]{0:T(128)} %bitcast.me_ref, bf16[256,4,256]{2,1,0:T(4,128)(2,1)S(1)} %bitcast.9), custom_call_target="tpu_custom_call" | custom-call | tf_op jit(solution)/shard_map/pallas_call | solution.py:94
  5.8 2.6 %collective-permute-start = (bf16[48,4,256]{2,1,0:T(4,128)(2,1)S(1)}, bf16[48,4,256]{2,1,0:T(4,128)(2,1)S(1)}, u32[]{:S(2)}, u32[]{:S(2)}) collective-permute-start(bf16[48,4,256]{2,1,0:T(4,128)(2,1)S(1)} %get-tuple-element.18), channel_id=1, source_target_pairs={{0,6},{1,7},{2,4},{3,5},{4,2},{5,3},{6,0},{7,1},{8,14},{9,15},{10,... | collective-permute-start | bytes 294920 | tf_op jit(solution)/shard_map/ppermute | solution.py:59
  8.4 0.5 %collective-permute-start.1 = (bf16[48,4,256]{2,1,0:T(4,128)(2,1)S(1)}, bf16[48,4,256]{2,1,0:T(4,128)(2,1)S(1)}, u32[]{:S(2)}, u32[]{:S(2)}) collective-permute-start(bf16[48,4,256]{2,1,0:T(4,128)(2,1)S(1)} %get-tuple-element.19), channel_id=1, source_target_pairs={{0,2},{1,3},{2,0},{3,1},{4,6},{5,7},{6,4},{7,5},{8,10},{9,11},{10,... | collective-permute-start | bytes 294920 | tf_op jit(solution)/shard_map/ppermute | solution.py:59
  8.9 0.8 %fusion.2 = bf16[2,8,4,256]{3,2,1,0:T(4,128)(2,1)S(1)} fusion(bf16[1,16,4,256]{3,2,1,0:T(4,128)(2,1)} %bitcast.12, bf16[1,16,4,256]{3,2,1,0:T(4,128)(2,1)S(1)} %bitcast.15, pred[]{:T(512)S(6)} %eq.3), kind=kLoop, calls=%fused_computation.7 | loop fusion | flops 49152 | bytes 98305 | tf_op jit(solution)/shard_map/jit(_where)/select_n | solution.py:198
  9.7 1.5 %collective-permute-start.5 = (bf16[2,8,4,256]{3,2,1,0:T(4,128)(2,1)S(1)}, bf16[2,8,4,256]{3,2,1,0:T(4,128)(2,1)S(1)}, u32[]{:S(2)}, u32[]{:S(2)}) collective-permute-start(bf16[2,8,4,256]{3,2,1,0:T(4,128)(2,1)S(1)} %fusion.2), channel_id=1, source_target_pairs={{0,6},{1,3},{2,0},{3,5},{4,2},{5,7},{6,4},{7,1},{8,14},{9,11},{10,... | collective-permute-start | bytes 98312 | tf_op jit(solution)/shard_map/ppermute | solution.py:68
  11.2 2.9 %collective-permute-done.5.edge_ref = bf16[2,8,4,256]{3,2,1,0:T(4,128)(2,1)S(1)} collective-permute-done((bf16[2,8,4,256]{3,2,1,0:T(4,128)(2,1)S(1)}, bf16[2,8,4,256]{3,2,1,0:T(4,128)(2,1)S(1)}, u32[]{:S(2)}, u32[]{:S(2)}) %collective-permute-start.5) | collective-permute-done | bytes 32800 | tf_op jit(solution)/shard_map/ppermute | solution.py:68
  14.1 1.3 %collective-permute-start.2 = (bf16[48,4,256]{2,1,0:T(4,128)(2,1)S(1)}, bf16[48,4,256]{2,1,0:T(4,128)(2,1)S(1)}, u32[]{:S(2)}, u32[]{:S(2)}) collective-permute-start(bf16[48,4,256]{2,1,0:T(4,128)(2,1)S(1)} %get-tuple-element.20), channel_id=1, source_target_pairs={{0,4},{1,5},{2,6},{3,7},{4,0},{5,1},{6,2},{7,3},{8,12},{9,13},{10,... | collective-permute-start | bytes 294920 | tf_op jit(solution)/shard_map/ppermute | solution.py:59
  15.4 0.4 %shard_map.29 = (bf16[48,4,256]{2,1,0:T(4,128)(2,1)S(1)}, bf16[48,4,256]{2,1,0:T(4,128)(2,1)S(1)}, bf16[48,4,256]{2,1,0:T(4,128)(2,1)S(1)}) custom-call(s32[1]{0:T(128)} %bitcast.me_ref, bf16[256,4,256]{2,1,0:T(4,128)(2,1)S(1)} %bitcast.10), custom_call_target="tpu_custom_call" | custom-call | tf_op jit(solution)/shard_map/pallas_call | solution.py:94
  15.8 0.8 %collective-permute-start.10 = (bf16[48,4,256]{2,1,0:T(4,128)(2,1)S(1)}, bf16[48,4,256]{2,1,0:T(4,128)(2,1)S(1)}, u32[]{:S(2)}, u32[]{:S(2)}) collective-permute-start(bf16[48,4,256]{2,1,0:T(4,128)(2,1)S(1)} %get-tuple-element.26), channel_id=1, source_target_pairs={{0,4},{1,5},{2,6},{3,7},{4,0},{5,1},{6,2},{7,3},{8,12},{9,13},{10,... | collective-permute-start | bytes 294920 | tf_op jit(solution)/shard_map/ppermute | solution.py:59
  16.6 1.9 %collective-permute-start.8 = (bf16[48,4,256]{2,1,0:T(4,128)(2,1)S(1)}, bf16[48,4,256]{2,1,0:T(4,128)(2,1)S(1)}, u32[]{:S(2)}, u32[]{:S(2)}) collective-permute-start(bf16[48,4,256]{2,1,0:T(4,128)(2,1)S(1)} %get-tuple-element.24), channel_id=1, source_target_pairs={{0,6},{1,7},{2,4},{3,5},{4,2},{5,3},{6,0},{7,1},{8,14},{9,15},{10,... | collective-permute-start | bytes 294920 | tf_op jit(solution)/shard_map/ppermute | solution.py:59
  18.5 0.9 %collective-permute-start.9 = (bf16[48,4,256]{2,1,0:T(4,128)(2,1)S(1)}, bf16[48,4,256]{2,1,0:T(4,128)(2,1)S(1)}, u32[]{:S(2)}, u32[]{:S(2)}) collective-permute-start(bf16[48,4,256]{2,1,0:T(4,128)(2,1)S(1)} %get-tuple-element.25), channel_id=1, source_target_pairs={{0,2},{1,3},{2,0},{3,1},{4,6},{5,7},{6,4},{7,5},{8,10},{9,11},{10,... | collective-permute-start | bytes 294920 | tf_op jit(solution)/shard_map/ppermute | solution.py:59
  19.5 0.3 collective-permute-done.2.d_ref
  19.8 0.9 %near.1 = (f32[16,4,256]{2,1,0:T(4,128)S(1)}, bf16[16,4,256]{2,1,0:T(4,128)(2,1)S(1)}) custom-call(s32[1]{0:T(128)} %bitcast.me_ref, bf16[48,4,256]{2,1,0:T(4,128)(2,1)S(1)} %get-tuple-element.17.a_ref, bf16[48,4,256]{2,1,0:T(4,128)(2,1)S(1)} %collective-permute-done.b_ref, bf16[48,4,256]{2,1,0:T(4,128)(2,1)S(1)} %collective-permute-done.1.c_ref, ...), custom_call_target="tpu_custom_call" | custom-call | tf_op jit(solution)/shard_map/near/pallas_call | solution.py:163
  20.7 0.3 collective-permute-start.7
  21.0 0.9 %collective-permute-done.10.d_ref = bf16[48,4,256]{2,1,0:T(4,128)(2,1)S(1)} collective-permute-done((bf16[48,4,256]{2,1,0:T(4,128)(2,1)S(1)}, bf16[48,4,256]{2,1,0:T(4,128)(2,1)S(1)}, u32[]{:S(2)}, u32[]{:S(2)}) %collective-permute-start.10) | collective-permute-done | bytes 98336 | tf_op jit(solution)/shard_map/ppermute | solution.py:59
  21.9 3.2 %collective-permute-done.8.b_ref = bf16[48,4,256]{2,1,0:T(4,128)(2,1)S(1)} collective-permute-done((bf16[48,4,256]{2,1,0:T(4,128)(2,1)S(1)}, bf16[48,4,256]{2,1,0:T(4,128)(2,1)S(1)}, u32[]{:S(2)}, u32[]{:S(2)}) %collective-permute-start.8) | collective-permute-done | bytes 98336 | tf_op jit(solution)/shard_map/ppermute | solution.py:59
  25.2 0.9 %far.1 = (bf16[16,4,256]{2,1,0:T(4,128)(2,1)S(1)}, bf16[16,4,256]{2,1,0:T(4,128)(2,1)S(1)}) custom-call(s32[1]{0:T(128)} %bitcast.me_ref, bf16[48,4,256]{2,1,0:T(4,128)(2,1)S(1)} %get-tuple-element.23.a_ref, bf16[48,4,256]{2,1,0:T(4,128)(2,1)S(1)} %collective-permute-done.8.b_ref, bf16[48,4,256]{2,1,0:T(4,128)(2,1)S(1)} %collective-permute-done.9.c_ref, ...), custom_call_target="tpu_custom_call" | custom-call | tf_op jit(solution)/shard_map/far/pallas_call | solution.py:163
  26.2 1.5 %collective-permute-start.12 = (bf16[16,4,256]{2,1,0:T(4,128)(2,1)S(1)}, bf16[16,4,256]{2,1,0:T(4,128)(2,1)S(1)}, u32[]{:S(2)}, u32[]{:S(2)}) collective-permute-start(bf16[16,4,256]{2,1,0:T(4,128)(2,1)S(1)} %get-tuple-element.27), channel_id=1, source_target_pairs={{0,8},{1,9},{2,10},{3,11},{4,12},{5,13},{6,14},{7,15},{8,0},{9,1},... | collective-permute-start | bytes 98312 | tf_op jit(solution)/shard_map/ppermute | solution.py:59
  27.7 0.3 collective-permute-start.13
  27.9 3.1 %collective-permute-done.12 = bf16[16,4,256]{2,1,0:T(4,128)(2,1)S(1)} collective-permute-done((bf16[16,4,256]{2,1,0:T(4,128)(2,1)S(1)}, bf16[16,4,256]{2,1,0:T(4,128)(2,1)S(1)}, u32[]{:S(2)}, u32[]{:S(2)}) %collective-permute-start.12) | collective-permute-done | bytes 32800 | tf_op jit(solution)/shard_map/ppermute | solution.py:59
  31.0 1.8 %collective-permute-done.13 = bf16[16,4,256]{2,1,0:T(4,128)(2,1)S(1)} collective-permute-done((bf16[16,4,256]{2,1,0:T(4,128)(2,1)S(1)}, bf16[16,4,256]{2,1,0:T(4,128)(2,1)S(1)}, u32[]{:S(2)}, u32[]{:S(2)}) %collective-permute-start.13) | collective-permute-done | bytes 32800 | tf_op jit(solution)/shard_map/ppermute | solution.py:59
  32.9 0.7 %fusion = bf16[16,4,1,256]{3,1,2,0:T(4,128)(2,1)} fusion(bf16[16,4,256]{2,1,0:T(4,128)(2,1)S(1)} %collective-permute-done.13, bf16[16,4,256]{2,1,0:T(4,128)(2,1)S(1)} %collective-permute-done.12, f32[16,4,256]{2,1,0:T(4,128)S(1)} %get-tuple-element.21, bf16[16,4,256]{2,1,0:T(4,128)(2,1)S(1)} %collective-permute-done.7), kind=kLoop, calls=%fused_computation.5 | loop fusion | flops 131072 | bytes 196608 | tf_op jit(solution)/shard_map/reshape | solution.py:210
  (17 shorter events, 0.3 us)
Async XLA Ops:
  0.0 8.9 %collective-permute-start.4 = (bf16[16,4,256]{2,1,0:T(4,128)(2,1)}, bf16[16,4,256]{2,1,0:T(4,128)(2,1)S(1)}, u32[]{:S(2)}, u32[]{:S(2)}) collective-permute-start(bf16[16,4,256]{2,1,0:T(4,128)(2,1)} %bitcast.11), channel_id=1, source_target_pairs={{0,8},{1,9},{2,10},{3,11},{4,12},{5,13},{6,14},{7,15},{8,0},{9,1},... | collective-permute-start | bytes 98312 | tf_op jit(solution)/shard_map/ppermute | solution.py:59
  4.1 1.0 %copy-start = (bf16[1,256,4,1,256]{4,2,3,1,0:T(4,128)(2,1)S(1)}, bf16[1,256,4,1,256]{4,2,3,1,0:T(4,128)(2,1)}, u32[]{:S(2)}) copy-start(bf16[1,256,4,1,256]{4,2,3,1,0:T(4,128)(2,1)} %param.2) | copy-start | bytes 1572868
  5.1 10.3 %copy-start.1 = (bf16[1,256,4,1,256]{4,2,3,1,0:T(4,128)(2,1)S(1)}, bf16[1,256,4,1,256]{4,2,3,1,0:T(4,128)(2,1)}, u32[]{:S(2)}) copy-start(bf16[1,256,4,1,256]{4,2,3,1,0:T(4,128)(2,1)} %param.2) | copy-start | bytes 1572868
  5.8 12.7 %collective-permute-start = (bf16[48,4,256]{2,1,0:T(4,128)(2,1)S(1)}, bf16[48,4,256]{2,1,0:T(4,128)(2,1)S(1)}, u32[]{:S(2)}, u32[]{:S(2)}) collective-permute-start(bf16[48,4,256]{2,1,0:T(4,128)(2,1)S(1)} %get-tuple-element.18), channel_id=1, source_target_pairs={{0,6},{1,7},{2,4},{3,5},{4,2},{5,3},{6,0},{7,1},{8,14},{9,15},{10,... | collective-permute-start | bytes 294920 | tf_op jit(solution)/shard_map/ppermute | solution.py:59
  8.4 11.0 %collective-permute-start.1 = (bf16[48,4,256]{2,1,0:T(4,128)(2,1)S(1)}, bf16[48,4,256]{2,1,0:T(4,128)(2,1)S(1)}, u32[]{:S(2)}, u32[]{:S(2)}) collective-permute-start(bf16[48,4,256]{2,1,0:T(4,128)(2,1)S(1)} %get-tuple-element.19), channel_id=1, source_target_pairs={{0,2},{1,3},{2,0},{3,1},{4,6},{5,7},{6,4},{7,5},{8,10},{9,11},{10,... | collective-permute-start | bytes 294920 | tf_op jit(solution)/shard_map/ppermute | solution.py:59
  8.9 2.3 %copy-start.2 = (bf16[16,4,1,256]{3,1,2,0:T(4,128)(2,1)S(1)}, bf16[16,4,1,256]{3,1,2,0:T(4,128)(2,1)}, u32[]{:S(2)}) copy-start(bf16[16,4,1,256]{3,1,2,0:T(4,128)(2,1)} %param.3) | copy-start | bytes 98308
  9.7 4.4 %collective-permute-start.5 = (bf16[2,8,4,256]{3,2,1,0:T(4,128)(2,1)S(1)}, bf16[2,8,4,256]{3,2,1,0:T(4,128)(2,1)S(1)}, u32[]{:S(2)}, u32[]{:S(2)}) collective-permute-start(bf16[2,8,4,256]{3,2,1,0:T(4,128)(2,1)S(1)} %fusion.2), channel_id=1, source_target_pairs={{0,6},{1,3},{2,0},{3,5},{4,2},{5,7},{6,4},{7,1},{8,14},{9,11},{10,... | collective-permute-start | bytes 98312 | tf_op jit(solution)/shard_map/ppermute | solution.py:68
  11.2 4.6 %collective-permute-start.3 = (bf16[16,4,256]{2,1,0:T(4,128)(2,1)S(1)}, bf16[16,4,256]{2,1,0:T(4,128)(2,1)S(1)}, u32[]{:S(2)}, u32[]{:S(2)}) collective-permute-start(bf16[16,4,256]{2,1,0:T(4,128)(2,1)S(1)} %bitcast.13), channel_id=1, source_target_pairs={{0,1},{1,0},{2,3},{3,2},{4,5},{5,4},{6,7},{7,6},{8,9},{9,8},{10,11... | collective-permute-start | bytes 98312 | tf_op jit(solution)/shard_map/ppermute | solution.py:59
  14.1 2.5 %collective-permute-start.6 = (bf16[2,8,4,256]{3,2,1,0:T(4,128)(2,1)S(1)}, bf16[2,8,4,256]{3,2,1,0:T(4,128)(2,1)S(1)}, u32[]{:S(2)}, u32[]{:S(2)}) collective-permute-start(bf16[2,8,4,256]{3,2,1,0:T(4,128)(2,1)S(1)} %collective-permute-done.5.edge_ref), channel_id=1, source_target_pairs={{0,1},{1,0},{2,3},{3,2},{4,5},{5,4},{6,7},{7,6},{8,9},{9,8},{10,11... | collective-permute-start | bytes 98312 | tf_op jit(solution)/shard_map/ppermute | solution.py:59
  14.1 5.7 %collective-permute-start.2 = (bf16[48,4,256]{2,1,0:T(4,128)(2,1)S(1)}, bf16[48,4,256]{2,1,0:T(4,128)(2,1)S(1)}, u32[]{:S(2)}, u32[]{:S(2)}) collective-permute-start(bf16[48,4,256]{2,1,0:T(4,128)(2,1)S(1)} %get-tuple-element.20), channel_id=1, source_target_pairs={{0,4},{1,5},{2,6},{3,7},{4,0},{5,1},{6,2},{7,3},{8,12},{9,13},{10,... | collective-permute-start | bytes 294920 | tf_op jit(solution)/shard_map/ppermute | solution.py:59
  15.8 6.1 %collective-permute-start.10 = (bf16[48,4,256]{2,1,0:T(4,128)(2,1)S(1)}, bf16[48,4,256]{2,1,0:T(4,128)(2,1)S(1)}, u32[]{:S(2)}, u32[]{:S(2)}) collective-permute-start(bf16[48,4,256]{2,1,0:T(4,128)(2,1)S(1)} %get-tuple-element.26), channel_id=1, source_target_pairs={{0,4},{1,5},{2,6},{3,7},{4,0},{5,1},{6,2},{7,3},{8,12},{9,13},{10,... | collective-permute-start | bytes 294920 | tf_op jit(solution)/shard_map/ppermute | solution.py:59
  16.6 8.5 %collective-permute-start.8 = (bf16[48,4,256]{2,1,0:T(4,128)(2,1)S(1)}, bf16[48,4,256]{2,1,0:T(4,128)(2,1)S(1)}, u32[]{:S(2)}, u32[]{:S(2)}) collective-permute-start(bf16[48,4,256]{2,1,0:T(4,128)(2,1)S(1)} %get-tuple-element.24), channel_id=1, source_target_pairs={{0,6},{1,7},{2,4},{3,5},{4,2},{5,3},{6,0},{7,1},{8,14},{9,15},{10,... | collective-permute-start | bytes 294920 | tf_op jit(solution)/shard_map/ppermute | solution.py:59
  18.5 6.7 %collective-permute-start.9 = (bf16[48,4,256]{2,1,0:T(4,128)(2,1)S(1)}, bf16[48,4,256]{2,1,0:T(4,128)(2,1)S(1)}, u32[]{:S(2)}, u32[]{:S(2)}) collective-permute-start(bf16[48,4,256]{2,1,0:T(4,128)(2,1)S(1)} %get-tuple-element.25), channel_id=1, source_target_pairs={{0,2},{1,3},{2,0},{3,1},{4,6},{5,7},{6,4},{7,5},{8,10},{9,11},{10,... | collective-permute-start | bytes 294920 | tf_op jit(solution)/shard_map/ppermute | solution.py:59
  19.4 1.6 %collective-permute-start.11 = (bf16[16,4,256]{2,1,0:T(4,128)(2,1)S(1)}, bf16[16,4,256]{2,1,0:T(4,128)(2,1)S(1)}, u32[]{:S(2)}, u32[]{:S(2)}) collective-permute-start(bf16[16,4,256]{2,1,0:T(4,128)(2,1)S(1)} %collective-permute-done.4.block_ref), channel_id=1, source_target_pairs={{0,1},{1,0},{2,3},{3,2},{4,5},{5,4},{6,7},{7,6},{8,9},{9,8},{10,11... | collective-permute-start | bytes 98312 | tf_op jit(solution)/shard_map/ppermute | solution.py:59
  20.7 7.2 %collective-permute-start.7 = (bf16[16,4,256]{2,1,0:T(4,128)(2,1)S(1)}, bf16[16,4,256]{2,1,0:T(4,128)(2,1)S(1)}, u32[]{:S(2)}, u32[]{:S(2)}) collective-permute-start(bf16[16,4,256]{2,1,0:T(4,128)(2,1)S(1)} %get-tuple-element.22), channel_id=1, source_target_pairs={{0,1},{1,0},{2,3},{3,2},{4,5},{5,4},{6,7},{7,6},{8,9},{9,8},{10,11... | collective-permute-start | bytes 98312 | tf_op jit(solution)/shard_map/ppermute | solution.py:59
  26.2 4.9 %collective-permute-start.12 = (bf16[16,4,256]{2,1,0:T(4,128)(2,1)S(1)}, bf16[16,4,256]{2,1,0:T(4,128)(2,1)S(1)}, u32[]{:S(2)}, u32[]{:S(2)}) collective-permute-start(bf16[16,4,256]{2,1,0:T(4,128)(2,1)S(1)} %get-tuple-element.27), channel_id=1, source_target_pairs={{0,8},{1,9},{2,10},{3,11},{4,12},{5,13},{6,14},{7,15},{8,0},{9,1},... | collective-permute-start | bytes 98312 | tf_op jit(solution)/shard_map/ppermute | solution.py:59
  27.7 5.2 %collective-permute-start.13 = (bf16[16,4,256]{2,1,0:T(4,128)(2,1)S(1)}, bf16[16,4,256]{2,1,0:T(4,128)(2,1)S(1)}, u32[]{:S(2)}, u32[]{:S(2)}) collective-permute-start(bf16[16,4,256]{2,1,0:T(4,128)(2,1)S(1)} %get-tuple-element.28), channel_id=1, source_target_pairs={{0,9},{1,8},{2,11},{3,10},{4,13},{5,12},{6,15},{7,14},{8,1},{9,0},... | collective-permute-start | bytes 98312 | tf_op jit(solution)/shard_map/ppermute | solution.py:59

commit v2 on v1

--- a/solution.py
+++ b/solution.py
@@ -10,7 +10,6 @@
 
 REACH = 8
 GRANT = 16 << 20
-FIRST_GRANT = 16 << 20
 
 
 def make_band(order):
@@ -53,18 +52,23 @@
 
 HALF, PAIR, SIDE, CORE = 8, 4, 2, 1
 PEERS = (PAIR + SIDE, SIDE, PAIR)
+SPLIT = (6, 2, 4)
+DIRECT = False
+CHAIN = True
 
 
 def swap(array, bits):
     return lax.ppermute(array, "mem", [(i, i ^ bits) for i in range(16)])
 
 
-def edges(array):
+def edges(array, bits=0):
     pairs = []
     for i in range(16):
-        half, place, core = i // 8, i // 2 % 4, i % 2
-        place = (place + (1 if core else 3)) % 4
-        pairs.append((i, half * 8 + place * 2 + core))
+        chip = i // 2 + (1 if i % 2 else -1)
+        if DIRECT and not 0 <= chip < 8:
+            continue
+        chip = chip if DIRECT else i // 8 * 4 + chip % 4
+        pairs.append((i, (2 * chip + i % 2) ^ bits))
     return lax.ppermute(array, "mem", pairs)
 
 
@@ -73,35 +77,47 @@
     return start, chip * strip - start
 
 
-def window_kernel(strip, wanted, me_ref, member_ref, *refs):
+def window_kernel(strip, wanted, me_ref, member_ref, grad_ref, *refs):
     outs, sem = refs[:-1], refs[-1]
     me = me_ref[0]
-    rows = member_ref.shape[0]
+    rows, part = member_ref.shape[0], grad_ref.shape[0]
     copies = []
+
+    def add(source, out):
+        copies.append(pltpu.make_async_copy(source, out, sem.at[len(copies)]))
+
     for bits, out in zip(wanted, outs):
-        start, _ = first_row(strip, (me ^ bits) // 2, rows)
-        copies.append(pltpu.make_async_copy(member_ref.at[pl.ds(start, strip + 2 * REACH)], out, sem.at[len(copies)]))
+        both = isinstance(bits, tuple)
+        for k, bit in enumerate(bits if both else (bits,)):
+            start, _ = first_row(strip, (me ^ bit) // 2, rows)
+            add(member_ref.at[pl.ds(start, strip + 2 * REACH)], out.at[k] if both else out)
+    add(grad_ref, outs[len(wanted)])
+    if DIRECT:
+        add(grad_ref.at[pl.ds((me % 2) * (part - REACH), REACH)], outs[len(wanted) + 1])
     for copy in copies:
         copy.start()
     for copy in copies:
         copy.wait()
 
 
-def windows(me, member, strip, wanted, grant):
+def windows(me, member, grad, strip, wanted):
     _, nvars, columns = member.shape
     shape = (strip + 2 * REACH, nvars, columns)
-    count = len(wanted)
+    outs = [jax.ShapeDtypeStruct((2,) + shape if isinstance(bits, tuple) else shape, member.dtype) for bits in wanted]
+    outs.append(jax.ShapeDtypeStruct(grad.shape, grad.dtype))
+    if DIRECT:
+        outs.append(jax.ShapeDtypeStruct((REACH,) + grad.shape[1:], grad.dtype))
     return pl.pallas_call(
         functools.partial(window_kernel, strip, wanted),
-        out_shape=[jax.ShapeDtypeStruct(shape, member.dtype)] * count,
-        in_specs=[pl.BlockSpec(memory_space=pltpu.SMEM), pl.BlockSpec(memory_space=pltpu.HBM)],
-        out_specs=[pl.BlockSpec(memory_space=pltpu.VMEM)] * count,
-        scratch_shapes=[pltpu.SemaphoreType.DMA((count,))],
-        compiler_params=pltpu.CompilerParams(vmem_limit_bytes=grant),
-    )(me, member)
-
-
-def strip_kernel(rows, far, me_ref, a_ref, b_ref, c_ref, d_ref, block_ref, mate_ref, edge_ref, edge_mate_ref, band_ref,
+        out_shape=outs,
+        in_specs=[pl.BlockSpec(memory_space=pltpu.SMEM)] + [pl.BlockSpec(memory_space=pltpu.HBM)] * 2,
+        out_specs=[pl.BlockSpec(memory_space=pltpu.VMEM)] * len(outs),
+        scratch_shapes=[pltpu.SemaphoreType.DMA((2 * len(outs),))],
+        compiler_params=pltpu.CompilerParams(vmem_limit_bytes=GRANT),
+    )(me, member, grad)
+
+
+def strip_kernel(rows, far, me_ref, a_ref, b_ref, c_ref, d_ref, block_ref, edge_ref, mate_ref, band_ref,
                  own_ref, other_ref, grad_ref, mixed_ref, total_ref):
     me = me_ref[0]
     core, place = me % 2, me // 2 % 4
@@ -114,13 +130,13 @@
 
     grad_ref[...] = jnp.zeros_like(grad_ref)
     grad_ref[pl.ds(at + core * part, part)] = block_ref[...]
-    grad_ref[pl.ds(at + (1 - core) * part, part)] = mate_ref[...]
-    before = jnp.where(place == 0, 1 - far, far)
-    after = jnp.where(place == 3, 1 - far, far)
+    grad_ref[pl.ds(at + (1 - core) * part, part)] = mate_ref[pl.ds(far * part, part)]
+    before = far if DIRECT else jnp.where(place == 0, 1 - far, far)
+    after = far if DIRECT else jnp.where(place == 3, 1 - far, far)
 
     @pl.when(jnp.logical_and(chip > 0, core == 0))
     def _():
-        grad_ref[pl.ds(at - reach, reach)] = edge_mate_ref[before]
+        grad_ref[pl.ds(at - reach, reach)] = mate_ref[pl.ds(2 * part + before * reach, reach)]
 
     @pl.when(jnp.logical_and(chip > 0, core == 1))
     def _():
@@ -132,10 +148,10 @@
 
     @pl.when(jnp.logical_and(chip < chips - 1, core == 1))
     def _():
-        grad_ref[pl.ds(at + strip, reach)] = edge_mate_ref[after]
+        grad_ref[pl.ds(at + strip, reach)] = mate_ref[pl.ds(2 * part + after * reach, reach)]
 
     grad = grad_ref[...].astype(jnp.float32)
-    members = (a_ref, b_ref, c_ref, d_ref)
+    members = [ref.at[far] if len(ref.shape) == 4 else ref for ref in (a_ref, b_ref, c_ref, d_ref)]
     for k, ref in enumerate(members):
         mixed = jnp.sum(ref[...].astype(jnp.float32) * grad, axis=1)
         mixed_ref[pl.ds(k * span, span)] = mixed.astype(jnp.bfloat16)
@@ -155,18 +171,19 @@
     other_ref[...] = total_ref[pl.ds((1 - core) * part, part)].astype(other_ref.dtype)
 
 
-def one_strip(me, members, block, mate, edge, edge_mate, band, rows, far):
-    span, nvars, columns = members[0].shape
+def one_strip(me, members, block, edge, mate, band, rows, far):
+    nvars, columns = block.shape[1:]
     part = block.shape[0]
+    span = 2 * part + 2 * edge.shape[1]
     piece = (part, nvars, columns)
     vmem = pl.BlockSpec(memory_space=pltpu.VMEM)
     return pl.pallas_call(
         functools.partial(strip_kernel, rows, far),
         out_shape=[
-            jax.ShapeDtypeStruct(piece, jnp.bfloat16 if far else jnp.float32),
+            jax.ShapeDtypeStruct(piece, jnp.float32 if CHAIN or not far else jnp.bfloat16),
             jax.ShapeDtypeStruct(piece, jnp.bfloat16),
         ],
-        in_specs=[pl.BlockSpec(memory_space=pltpu.SMEM)] + [vmem] * 9,
+        in_specs=[pl.BlockSpec(memory_space=pltpu.SMEM)] + [vmem] * 8,
         out_specs=[vmem] * 2,
         scratch_shapes=[
             pltpu.VMEM((span, nvars, columns), jnp.bfloat16),
@@ -175,7 +192,7 @@
         ],
         compiler_params=pltpu.CompilerParams(vmem_limit_bytes=GRANT),
         name="far" if far else "near",
-    )(me, *members, block, mate, edge, edge_mate, band)
+    )(me, *members, block, edge, mate, band)
 
 
 def by_halves(perturbations, gradient):
@@ -185,28 +202,46 @@
     members = lax.axis_size("mem")
     at = lax.axis_index("mem")
     me = at.reshape(1).astype(jnp.int32)
-    here = gradient.reshape(local_rows, nvars, columns)
-    member = perturbations.reshape(-1, nvars, columns)
-
-    far_out = windows(me, member, strip, [p ^ HALF for p in PEERS], FIRST_GRANT)
-    far_in = [swap(block, p) for block, p in zip(far_out, PEERS)]
+    param = gradient.reshape(local_rows, nvars, columns)
+    member = pltpu.with_memory_space_constraint(perturbations.reshape(-1, nvars, columns), pltpu.HBM)
+    stays = pltpu.with_memory_space_constraint(param, pltpu.HBM)
+
+    wanted = []
+    for p in PEERS:
+        wanted += [p ^ HALF, p] if p in SPLIT else [(p, p ^ HALF)]
+    out = list(windows(me, member, stays, strip, wanted + [(0, HALF)]))
+    mine, here = out[len(wanted)], out[len(wanted) + 1]
+    edge_out = out[-1]
+    far_in, near_in = [mine], [mine]
+    for p in PEERS:
+        if p in SPLIT:
+            far_in.append(swap(out.pop(0), p))
+            near_in.append(swap(out.pop(0), p))
+        else:
+            both = swap(out.pop(0), p)
+            far_in.append(both)
+            near_in.append(both)
     there = swap(here, HALF)
-    *near_out, near_mine, far_mine = windows(me, member, strip, list(PEERS) + [0, HALF], GRANT)
-    near_in = [swap(block, p) for block, p in zip(near_out, PEERS)]
-    here_mate = swap(here, CORE)
-    both = jnp.stack([here, there])
-    both = jnp.where(at & 1 == 0, both[:, :REACH], both[:, -REACH:])
-    edge = edges(both)
-    there_mate = swap(there, CORE)
-    edge_mate = swap(edge, CORE)
+    if DIRECT:
+        edge = jnp.stack([edges(edge_out), edges(edge_out, HALF)])
+    else:
+        both = jnp.stack([here, there])
+        both = jnp.where(at & 1 == 0, both[:, :REACH], both[:, -REACH:])
+        edge = edges(both)
+    mate = swap(jnp.concatenate([here, there, edge[0], edge[1]]), CORE)
 
     band = make_band(columns)
-    args = (edge, edge_mate, band, grid_rows)
-    far_own, far_other = one_strip(me, [far_mine] + far_in, there, there_mate, *args, 1)
-    far_own, far_other = swap(far_own, HALF), swap(far_other, HALF + CORE)
-    near_own, near_other = one_strip(me, [near_mine] + near_in, here, here_mate, *args, 0)
+    args = (edge, mate, band, grid_rows)
+    far_own, far_other = one_strip(me, far_in, there, *args, 1)
+    if CHAIN:
+        far_sum = far_own + swap(far_other, CORE).astype(jnp.float32)
+        far_sum = swap(far_sum.astype(jnp.bfloat16), HALF).astype(jnp.float32)
+    else:
+        far_own, far_other = swap(far_own, HALF), swap(far_other, HALF + CORE)
+        far_sum = far_own.astype(jnp.float32) + far_other.astype(jnp.float32)
+    near_own, near_other = one_strip(me, near_in, here, *args, 0)
     near_other = swap(near_other, CORE)
-    total = near_own + near_other.astype(jnp.float32) + far_own.astype(jnp.float32) + far_other.astype(jnp.float32)
+    total = near_own + near_other.astype(jnp.float32) + far_sum
     return (total * (1.0 / (members - 1))).astype(jnp.bfloat16).reshape(gradient.shape)
 
 

time: 33.7 us -> 32.7 us (0.970)
  local copies, waits for them, and re-layouts: 1.05 us -> 0.01 us
  starting transfers between devices: 15.5 us -> 16.5 us
  other arithmetic: 1.59 us -> 0.89 us
  waiting for transfers between devices: 12.4 us -> 11.8 us
    ppermute x1, waiting for transfers between devices: 2.92 us -> 0.01 us  [edges(): return lax.ppermute(array, 'mem', pairs)]
    ppermute x13 -> x11, waiting for transfers between devices: 9.49 us -> 11.8 us  [swap(): return lax.ppermute(array, 'mem', [(i, i ^ bits) for i in range(16)])]
    ppermute x1, starting transfers between devices: 1.46 us -> 2.56 us  [edges(): return lax.ppermute(array, 'mem', pairs)]
    unnamed x6 -> x0, local copies, waits for them, and re-layouts: 1.05 us -> none
    select_n x1, other arithmetic: 0.83 us -> 0.04 us  [by_halves(): both = jnp.where(at & 1 == 0, both[:, :REACH], both[:, -REACH:])]
    pallas_call x2 -> x1, Pallas kernels: 1.05 us -> 1.35 us  [windows(): pl.pallas_call(functools.partial(window_kernel, strip, wanted), out_shape...]
    ppermute x13 -> x11, starting transfers between devices: 14.1 us -> 13.9 us  [swap(): return lax.ppermute(array, 'mem', [(i, i ^ bits) for i in range(16)])]
  transfers between devices with their start and end apart: 14 -> 12, of which waited for: 7 -> 5; matrix products, arithmetic and copies ran while one was open for 3% -> 1% of each run, Pallas kernels for 9% -> 6%
where the time goes in v2:
time: 32.7 us; the launch traced here: 32.5 us
  starting transfers between devices  16.5 us (50%)
  waiting for transfers between devices  11.8 us (36%)
  Pallas kernels  3.2 us (10%)
  other arithmetic  0.89 us (3%)
    ppermute x11, starting transfers between devices, swap(): return lax.ppermute(array, 'mem', [(i, i ^ bits) for i in range(16)])  13.9 us
    ppermute x11, waiting for transfers between devices, swap(): return lax.ppermute(array, 'mem', [(i, i ^ bits) for i in range(16)])  11.8 us
    ppermute x1, starting transfers between devices, edges(): return lax.ppermute(array, 'mem', pairs)  2.56 us
    pallas_call x2, Pallas kernels, one_strip(): pl.pallas_call(functools.partial(strip_kernel, rows, far), out_shape=[jax...  1.85 us
    pallas_call x1, Pallas kernels, windows(): pl.pallas_call(functools.partial(window_kernel, strip, wanted), out_shape...  1.35 us
  transfers between devices with their start and end apart: 12, of which 5 were waited for; matrix products, arithmetic and copies ran while one was open for 1% of the time, Pallas kernels for 6%

profile of v2, /device:TPU:0, one launch (start us, length us, event | category | flops | bytes accessed | tf_op | source)
XLA Modules:
  0.0 32.5 jit_solution(12177965588946519009)
XLA Ops:
  0.0 1.4 %shard_map.28 = (bf16[48,4,256]{2,1,0:T(4,128)(2,1)S(1)}, bf16[48,4,256]{2,1,0:T(4,128)(2,1)S(1)}, bf16[48,4,256]{2,1,0:T(4,128)(2,1)S(1)}, bf16[48,4,256]{2,1,0...) custom-call(s32[1]{0:T(128)} %bitcast.me_ref, ...), custom_call_target="tpu_custom_call" | custom-call | tf_op jit(solution)/shard_map/pallas_call | solution.py:110
  1.4 4.1 %collective-permute-start.3 = (bf16[16,4,256]{2,1,0:T(4,128)(2,1)S(1)}, bf16[16,4,256]{2,1,0:T(4,128)(2,1)S(1)}, u32[]{:S(2)}, u32[]{:S(2)}) collective-permute-start(bf16[16,4,256]{2,1,0:T(4,128)(2,1)S(1)} %get-tuple-element.21.block_ref), channel_id=1, source_target_pairs={{0,8},{1,9},{2,10},{3,11},{4,12},{5,13},{6,14},{7,15},{8,0},{9,1},... | collective-permute-start | bytes 98312 | tf_op jit(solution)/shard_map/ppermute | solution.py:61
  5.5 2.2 %collective-permute-done.3.block_ref = bf16[16,4,256]{2,1,0:T(4,128)(2,1)S(1)} collective-permute-done((bf16[16,4,256]{2,1,0:T(4,128)(2,1)S(1)}, bf16[16,4,256]{2,1,0:T(4,128)(2,1)S(1)}, u32[]{:S(2)}, u32[]{:S(2)}) %collective-permute-start.3) | collective-permute-done | bytes 32800 | tf_op jit(solution)/shard_map/ppermute | solution.py:61
  7.8 2.6 %collective-permute-start.4 = (bf16[2,8,4,256]{3,2,1,0:T(4,128)(2,1)S(1)}, bf16[2,8,4,256]{3,2,1,0:T(4,128)(2,1)S(1)}, u32[]{:S(2)}, u32[]{:S(2)}) collective-permute-start(bf16[2,8,4,256]{3,2,1,0:T(4,128)(2,1)S(1)} %fusion.2), channel_id=1, source_target_pairs={{0,6},{1,3},{2,0},{3,5},{4,2},{5,7},{6,4},{7,1},{8,14},{9,11},{10,... | collective-permute-start | bytes 98312 | tf_op jit(solution)/shard_map/ppermute | solution.py:72
  10.3 0.5 %collective-permute-start = (bf16[48,4,256]{2,1,0:T(4,128)(2,1)S(1)}, bf16[48,4,256]{2,1,0:T(4,128)(2,1)S(1)}, u32[]{:S(2)}, u32[]{:S(2)}) collective-permute-start(bf16[48,4,256]{2,1,0:T(4,128)(2,1)S(1)} %get-tuple-element.18), channel_id=1, source_target_pairs={{0,6},{1,7},{2,4},{3,5},{4,2},{5,3},{6,0},{7,1},{8,14},{9,15},{10,... | collective-permute-start | bytes 294920 | tf_op jit(solution)/shard_map/ppermute | solution.py:61
  10.9 1.6 %collective-permute-start.1 = (bf16[48,4,256]{2,1,0:T(4,128)(2,1)S(1)}, bf16[48,4,256]{2,1,0:T(4,128)(2,1)S(1)}, u32[]{:S(2)}, u32[]{:S(2)}) collective-permute-start(bf16[48,4,256]{2,1,0:T(4,128)(2,1)S(1)} %get-tuple-element.19), channel_id=1, source_target_pairs={{0,2},{1,3},{2,0},{3,1},{4,6},{5,7},{6,4},{7,5},{8,10},{9,11},{10,... | collective-permute-start | bytes 294920 | tf_op jit(solution)/shard_map/ppermute | solution.py:61
  12.5 1.3 %collective-permute-start.2 = (bf16[48,4,256]{2,1,0:T(4,128)(2,1)S(1)}, bf16[48,4,256]{2,1,0:T(4,128)(2,1)S(1)}, u32[]{:S(2)}, u32[]{:S(2)}) collective-permute-start(bf16[48,4,256]{2,1,0:T(4,128)(2,1)S(1)} %get-tuple-element.20), channel_id=1, source_target_pairs={{0,4},{1,5},{2,6},{3,7},{4,0},{5,1},{6,2},{7,3},{8,12},{9,13},{10,... | collective-permute-start | bytes 294920 | tf_op jit(solution)/shard_map/ppermute | solution.py:61
  13.8 0.5 %collective-permute-start.7 = (bf16[48,4,256]{2,1,0:T(4,128)(2,1)S(1)}, bf16[48,4,256]{2,1,0:T(4,128)(2,1)S(1)}, u32[]{:S(2)}, u32[]{:S(2)}) collective-permute-start(bf16[48,4,256]{2,1,0:T(4,128)(2,1)S(1)} %get-tuple-element.24), channel_id=1, source_target_pairs={{0,6},{1,7},{2,4},{3,5},{4,2},{5,3},{6,0},{7,1},{8,14},{9,15},{10,... | collective-permute-start | bytes 294920 | tf_op jit(solution)/shard_map/ppermute | solution.py:61
  14.3 0.0 collective-permute-done.4.edge_ref
  14.3 1.6 %collective-permute-start.8 = (bf16[48,4,256]{2,1,0:T(4,128)(2,1)S(1)}, bf16[48,4,256]{2,1,0:T(4,128)(2,1)S(1)}, u32[]{:S(2)}, u32[]{:S(2)}) collective-permute-start(bf16[48,4,256]{2,1,0:T(4,128)(2,1)S(1)} %get-tuple-element.25), channel_id=1, source_target_pairs={{0,2},{1,3},{2,0},{3,1},{4,6},{5,7},{6,4},{7,5},{8,10},{9,11},{10,... | collective-permute-start | bytes 294920 | tf_op jit(solution)/shard_map/ppermute | solution.py:61
  16.0 0.1 pad_maximum_fusion
  16.1 3.4 %collective-permute-done.7.b_ref = bf16[48,4,256]{2,1,0:T(4,128)(2,1)S(1)} collective-permute-done((bf16[48,4,256]{2,1,0:T(4,128)(2,1)S(1)}, bf16[48,4,256]{2,1,0:T(4,128)(2,1)S(1)}, u32[]{:S(2)}, u32[]{:S(2)}) %collective-permute-start.7) | collective-permute-done | bytes 98336 | tf_op jit(solution)/shard_map/ppermute | solution.py:61
  19.5 0.7 %collective-permute-start.9 = (bf16[48,4,256]{2,1,0:T(4,128)(2,1)S(1)}, bf16[48,4,256]{2,1,0:T(4,128)(2,1)S(1)}, u32[]{:S(2)}, u32[]{:S(2)}) collective-permute-start(bf16[48,4,256]{2,1,0:T(4,128)(2,1)S(1)} %get-tuple-element.26), channel_id=1, source_target_pairs={{0,4},{1,5},{2,6},{3,7},{4,0},{5,1},{6,2},{7,3},{8,12},{9,13},{10,... | collective-permute-start | bytes 294920 | tf_op jit(solution)/shard_map/ppermute | solution.py:61
  20.1 0.1 collective-permute-done.8.c_ref
  20.2 0.0 collective-permute-start.5
  20.2 0.1 select_convert_fusion.band_ref
  20.3 3.8 %collective-permute-done.9.d_ref = bf16[48,4,256]{2,1,0:T(4,128)(2,1)S(1)} collective-permute-done((bf16[48,4,256]{2,1,0:T(4,128)(2,1)S(1)}, bf16[48,4,256]{2,1,0:T(4,128)(2,1)S(1)}, u32[]{:S(2)}, u32[]{:S(2)}) %collective-permute-start.9) | collective-permute-done | bytes 98336 | tf_op jit(solution)/shard_map/ppermute | solution.py:61
  24.1 0.9 %far.1 = (f32[16,4,256]{2,1,0:T(4,128)S(1)}, bf16[16,4,256]{2,1,0:T(4,128)(2,1)S(1)}) custom-call(s32[1]{0:T(128)} %bitcast.me_ref, bf16[2,48,4,256]{3,2,1,0:T(4,128)(2,1)S(1)} %get-tuple-element.17.a_ref, bf16[48,4,256]{2,1,0:T(4,128)(2,1)S(1)} %collective-permute-done.7.b_ref, bf16[48,4,256]{2,1,0:T(4,128)(2,1)S(1)} %collective-permute-done.8.c_ref, ...), custom_call_target="tpu_custom_call" | custom-call | tf_op jit(solution)/shard_map/far/pallas_call | solution.py:180
  25.0 0.1 collective-permute-start.10
  25.1 0.9 %near.1 = (f32[16,4,256]{2,1,0:T(4,128)S(1)}, bf16[16,4,256]{2,1,0:T(4,128)(2,1)S(1)}) custom-call(s32[1]{0:T(128)} %bitcast.me_ref, bf16[2,48,4,256]{3,2,1,0:T(4,128)(2,1)S(1)} %get-tuple-element.17.a_ref, bf16[48,4,256]{2,1,0:T(4,128)(2,1)S(1)} %collective-permute-done.b_ref, bf16[48,4,256]{2,1,0:T(4,128)(2,1)S(1)} %collective-permute-done.1.c_ref, ...), custom_call_target="tpu_custom_call" | custom-call | tf_op jit(solution)/shard_map/near/pallas_call | solution.py:180
  26.1 0.5 %collective-permute-start.6 = (bf16[16,4,256]{2,1,0:T(4,128)(2,1)S(1)}, bf16[16,4,256]{2,1,0:T(4,128)(2,1)S(1)}, u32[]{:S(2)}, u32[]{:S(2)}) collective-permute-start(bf16[16,4,256]{2,1,0:T(4,128)(2,1)S(1)} %get-tuple-element.23), channel_id=1, source_target_pairs={{0,1},{1,0},{2,3},{3,2},{4,5},{5,4},{6,7},{7,6},{8,9},{9,8},{10,11... | collective-permute-start | bytes 98312 | tf_op jit(solution)/shard_map/ppermute | solution.py:61
  26.6 2.9 %collective-permute-start.11 = (bf16[16,4,256]{2,1,0:T(4,128)(2,1)S(1)}, bf16[16,4,256]{2,1,0:T(4,128)(2,1)S(1)}, u32[]{:S(2)}, u32[]{:S(2)}) collective-permute-start(bf16[16,4,256]{2,1,0:T(4,128)(2,1)S(1)} %add_convert_fusion), channel_id=1, source_target_pairs={{0,8},{1,9},{2,10},{3,11},{4,12},{5,13},{6,14},{7,15},{8,0},{9,1},... | collective-permute-start | bytes 98312 | tf_op jit(solution)/shard_map/ppermute | solution.py:61
  29.5 2.3 %collective-permute-done.11 = bf16[16,4,256]{2,1,0:T(4,128)(2,1)S(1)} collective-permute-done((bf16[16,4,256]{2,1,0:T(4,128)(2,1)S(1)}, bf16[16,4,256]{2,1,0:T(4,128)(2,1)S(1)}, u32[]{:S(2)}, u32[]{:S(2)}) %collective-permute-start.11) | collective-permute-done | bytes 32800 | tf_op jit(solution)/shard_map/ppermute | solution.py:61
  31.9 0.6 %fusion = bf16[16,4,1,256]{3,1,2,0:T(4,128)(2,1)} fusion(bf16[16,4,256]{2,1,0:T(4,128)(2,1)S(1)} %collective-permute-done.11, f32[16,4,256]{2,1,0:T(4,128)S(1)} %get-tuple-element.22, bf16[16,4,256]{2,1,0:T(4,128)(2,1)S(1)} %collective-permute-done.6), kind=kLoop, calls=%fused_computation.7 | loop fusion | flops 98304 | bytes 163840 | tf_op jit(solution)/shard_map/reshape | solution.py:245
  (9 shorter events, 0.1 us)
Async XLA Ops:
  1.4 6.4 %collective-permute-start.3 = (bf16[16,4,256]{2,1,0:T(4,128)(2,1)S(1)}, bf16[16,4,256]{2,1,0:T(4,128)(2,1)S(1)}, u32[]{:S(2)}, u32[]{:S(2)}) collective-permute-start(bf16[16,4,256]{2,1,0:T(4,128)(2,1)S(1)} %get-tuple-element.21.block_ref), channel_id=1, source_target_pairs={{0,8},{1,9},{2,10},{3,11},{4,12},{5,13},{6,14},{7,15},{8,0},{9,1},... | collective-permute-start | bytes 98312 | tf_op jit(solution)/shard_map/ppermute | solution.py:61
  7.8 6.6 %collective-permute-start.4 = (bf16[2,8,4,256]{3,2,1,0:T(4,128)(2,1)S(1)}, bf16[2,8,4,256]{3,2,1,0:T(4,128)(2,1)S(1)}, u32[]{:S(2)}, u32[]{:S(2)}) collective-permute-start(bf16[2,8,4,256]{3,2,1,0:T(4,128)(2,1)S(1)} %fusion.2), channel_id=1, source_target_pairs={{0,6},{1,3},{2,0},{3,5},{4,2},{5,7},{6,4},{7,1},{8,14},{9,11},{10,... | collective-permute-start | bytes 98312 | tf_op jit(solution)/shard_map/ppermute | solution.py:72
  10.3 14.7 %collective-permute-start = (bf16[48,4,256]{2,1,0:T(4,128)(2,1)S(1)}, bf16[48,4,256]{2,1,0:T(4,128)(2,1)S(1)}, u32[]{:S(2)}, u32[]{:S(2)}) collective-permute-start(bf16[48,4,256]{2,1,0:T(4,128)(2,1)S(1)} %get-tuple-element.18), channel_id=1, source_target_pairs={{0,6},{1,7},{2,4},{3,5},{4,2},{5,3},{6,0},{7,1},{8,14},{9,15},{10,... | collective-permute-start | bytes 294920 | tf_op jit(solution)/shard_map/ppermute | solution.py:61
  10.9 14.2 %collective-permute-start.1 = (bf16[48,4,256]{2,1,0:T(4,128)(2,1)S(1)}, bf16[48,4,256]{2,1,0:T(4,128)(2,1)S(1)}, u32[]{:S(2)}, u32[]{:S(2)}) collective-permute-start(bf16[48,4,256]{2,1,0:T(4,128)(2,1)S(1)} %get-tuple-element.19), channel_id=1, source_target_pairs={{0,2},{1,3},{2,0},{3,1},{4,6},{5,7},{6,4},{7,5},{8,10},{9,11},{10,... | collective-permute-start | bytes 294920 | tf_op jit(solution)/shard_map/ppermute | solution.py:61
  12.5 12.6 %collective-permute-start.2 = (bf16[48,4,256]{2,1,0:T(4,128)(2,1)S(1)}, bf16[48,4,256]{2,1,0:T(4,128)(2,1)S(1)}, u32[]{:S(2)}, u32[]{:S(2)}) collective-permute-start(bf16[48,4,256]{2,1,0:T(4,128)(2,1)S(1)} %get-tuple-element.20), channel_id=1, source_target_pairs={{0,4},{1,5},{2,6},{3,7},{4,0},{5,1},{6,2},{7,3},{8,12},{9,13},{10,... | collective-permute-start | bytes 294920 | tf_op jit(solution)/shard_map/ppermute | solution.py:61
  13.8 5.6 %collective-permute-start.7 = (bf16[48,4,256]{2,1,0:T(4,128)(2,1)S(1)}, bf16[48,4,256]{2,1,0:T(4,128)(2,1)S(1)}, u32[]{:S(2)}, u32[]{:S(2)}) collective-permute-start(bf16[48,4,256]{2,1,0:T(4,128)(2,1)S(1)} %get-tuple-element.24), channel_id=1, source_target_pairs={{0,6},{1,7},{2,4},{3,5},{4,2},{5,3},{6,0},{7,1},{8,14},{9,15},{10,... | collective-permute-start | bytes 294920 | tf_op jit(solution)/shard_map/ppermute | solution.py:61
  14.3 5.9 %collective-permute-start.8 = (bf16[48,4,256]{2,1,0:T(4,128)(2,1)S(1)}, bf16[48,4,256]{2,1,0:T(4,128)(2,1)S(1)}, u32[]{:S(2)}, u32[]{:S(2)}) collective-permute-start(bf16[48,4,256]{2,1,0:T(4,128)(2,1)S(1)} %get-tuple-element.25), channel_id=1, source_target_pairs={{0,2},{1,3},{2,0},{3,1},{4,6},{5,7},{6,4},{7,5},{8,10},{9,11},{10,... | collective-permute-start | bytes 294920 | tf_op jit(solution)/shard_map/ppermute | solution.py:61
  19.5 4.6 %collective-permute-start.9 = (bf16[48,4,256]{2,1,0:T(4,128)(2,1)S(1)}, bf16[48,4,256]{2,1,0:T(4,128)(2,1)S(1)}, u32[]{:S(2)}, u32[]{:S(2)}) collective-permute-start(bf16[48,4,256]{2,1,0:T(4,128)(2,1)S(1)} %get-tuple-element.26), channel_id=1, source_target_pairs={{0,4},{1,5},{2,6},{3,7},{4,0},{5,1},{6,2},{7,3},{8,12},{9,13},{10,... | collective-permute-start | bytes 294920 | tf_op jit(solution)/shard_map/ppermute | solution.py:61
  20.2 3.9 %collective-permute-start.5 = (bf16[48,4,256]{2,1,0:T(4,128)(2,1)S(1)}, bf16[48,4,256]{2,1,0:T(4,128)(2,1)S(1)}, u32[]{:S(2)}, u32[]{:S(2)}) collective-permute-start(bf16[48,4,256]{2,1,0:T(4,128)(2,1)S(1)} %pad_maximum_fusion), channel_id=1, source_target_pairs={{0,1},{1,0},{2,3},{3,2},{4,5},{5,4},{6,7},{7,6},{8,9},{9,8},{10,11... | collective-permute-start | bytes 294920 | tf_op jit(solution)/shard_map/ppermute | solution.py:61
  25.0 1.6 %collective-permute-start.10 = (bf16[16,4,256]{2,1,0:T(4,128)(2,1)S(1)}, bf16[16,4,256]{2,1,0:T(4,128)(2,1)S(1)}, u32[]{:S(2)}, u32[]{:S(2)}) collective-permute-start(bf16[16,4,256]{2,1,0:T(4,128)(2,1)S(1)} %get-tuple-element.28), channel_id=1, source_target_pairs={{0,1},{1,0},{2,3},{3,2},{4,5},{5,4},{6,7},{7,6},{8,9},{9,8},{10,11... | collective-permute-start | bytes 98312 | tf_op jit(solution)/shard_map/ppermute | solution.py:61
  26.1 3.5 %collective-permute-start.6 = (bf16[16,4,256]{2,1,0:T(4,128)(2,1)S(1)}, bf16[16,4,256]{2,1,0:T(4,128)(2,1)S(1)}, u32[]{:S(2)}, u32[]{:S(2)}) collective-permute-start(bf16[16,4,256]{2,1,0:T(4,128)(2,1)S(1)} %get-tuple-element.23), channel_id=1, source_target_pairs={{0,1},{1,0},{2,3},{3,2},{4,5},{5,4},{6,7},{7,6},{8,9},{9,8},{10,11... | collective-permute-start | bytes 98312 | tf_op jit(solution)/shard_map/ppermute | solution.py:61
  26.6 5.2 %collective-permute-start.11 = (bf16[16,4,256]{2,1,0:T(4,128)(2,1)S(1)}, bf16[16,4,256]{2,1,0:T(4,128)(2,1)S(1)}, u32[]{:S(2)}, u32[]{:S(2)}) collective-permute-start(bf16[16,4,256]{2,1,0:T(4,128)(2,1)S(1)} %add_convert_fusion), channel_id=1, source_target_pairs={{0,8},{1,9},{2,10},{3,11},{4,12},{5,13},{6,14},{7,15},{8,0},{9,1},... | collective-permute-start | bytes 98312 | tf_op jit(solution)/shard_map/ppermute | solution.py:61

commit v3 on v2

--- a/solution.py
+++ b/solution.py
@@ -80,7 +80,7 @@
 def window_kernel(strip, wanted, me_ref, member_ref, grad_ref, *refs):
     outs, sem = refs[:-1], refs[-1]
     me = me_ref[0]
-    rows, part = member_ref.shape[0], grad_ref.shape[0]
+    rows = member_ref.shape[0]
     copies = []
 
     def add(source, out):
@@ -91,22 +91,20 @@
         for k, bit in enumerate(bits if both else (bits,)):
             start, _ = first_row(strip, (me ^ bit) // 2, rows)
             add(member_ref.at[pl.ds(start, strip + 2 * REACH)], out.at[k] if both else out)
-    add(grad_ref, outs[len(wanted)])
-    if DIRECT:
-        add(grad_ref.at[pl.ds((me % 2) * (part - REACH), REACH)], outs[len(wanted) + 1])
+    if len(outs) > len(wanted):
+        add(grad_ref, outs[len(wanted)])
     for copy in copies:
         copy.start()
     for copy in copies:
         copy.wait()
 
 
-def windows(me, member, grad, strip, wanted):
+def windows(me, member, grad, strip, wanted, keep=True):
     _, nvars, columns = member.shape
     shape = (strip + 2 * REACH, nvars, columns)
     outs = [jax.ShapeDtypeStruct((2,) + shape if isinstance(bits, tuple) else shape, member.dtype) for bits in wanted]
-    outs.append(jax.ShapeDtypeStruct(grad.shape, grad.dtype))
-    if DIRECT:
-        outs.append(jax.ShapeDtypeStruct((REACH,) + grad.shape[1:], grad.dtype))
+    if keep:
+        outs.append(jax.ShapeDtypeStruct(grad.shape, grad.dtype))
     return pl.pallas_call(
         functools.partial(window_kernel, strip, wanted),
         out_shape=outs,
@@ -152,8 +150,16 @@
 
     grad = grad_ref[...].astype(jnp.float32)
     members = [ref.at[far] if len(ref.shape) == 4 else ref for ref in (a_ref, b_ref, c_ref, d_ref)]
+    nvars, columns = grad.shape[1:]
+    grad = grad.reshape(span * nvars, columns)
+    row = lax.broadcasted_iota(jnp.int32, (span, span * nvars), 1) // nvars
+    pick = jnp.where(row == lax.broadcasted_iota(jnp.int32, row.shape, 0), 1.0, 0.0).astype(jnp.bfloat16)
     for k, ref in enumerate(members):
-        mixed = jnp.sum(ref[...].astype(jnp.float32) * grad, axis=1)
+        terms = ref[...].reshape(span * nvars, columns).astype(jnp.float32) * grad
+        high = terms.astype(jnp.bfloat16)
+        low = (terms - high.astype(jnp.float32)).astype(jnp.bfloat16)
+        mixed = jnp.dot(pick, high, preferred_element_type=jnp.float32)
+        mixed = mixed + jnp.dot(pick, low, preferred_element_type=jnp.float32)
         mixed_ref[pl.ds(k * span, span)] = mixed.astype(jnp.bfloat16)
     along = jnp.dot(mixed_ref[...], band_ref[...], preferred_element_type=jnp.float32).astype(jnp.bfloat16)
     offset = lax.broadcasted_iota(jnp.int32, (strip, span), 0) + at - lax.broadcasted_iota(jnp.int32, (strip, span), 1)
@@ -209,9 +215,13 @@
     wanted = []
     for p in PEERS:
         wanted += [p ^ HALF, p] if p in SPLIT else [(p, p ^ HALF)]
-    out = list(windows(me, member, stays, strip, wanted + [(0, HALF)]))
-    mine, here = out[len(wanted)], out[len(wanted) + 1]
-    edge_out = out[-1]
+    wanted.append((0, HALF))
+    cut = 99
+    out = list(windows(me, member, stays, strip, wanted[:cut]))
+    here = out.pop()
+    if cut < len(wanted):
+        out += windows(me, member, stays, strip, wanted[cut:], False)
+    mine = out[-1]
     far_in, near_in = [mine], [mine]
     for p in PEERS:
         if p in SPLIT:
@@ -221,7 +231,7 @@
             both = swap(out.pop(0), p)
             far_in.append(both)
             near_in.append(both)
-    there = swap(here, HALF)
+    there = swap(param, HALF)
     if DIRECT:
         edge = jnp.stack([edges(edge_out), edges(edge_out, HALF)])
     else:

time: 32.7 us -> 31 us (0.948)
  waiting for transfers between devices: 11.8 us -> 10.6 us
  Pallas kernels: 3.2 us -> 2.77 us
    ppermute x11, waiting for transfers between devices: 11.8 us -> 10.6 us  [swap(): return lax.ppermute(array, 'mem', [(i, i ^ bits) for i in range(16)])]
    pallas_call x2, Pallas kernels: 1.85 us -> 1.42 us  [one_strip(): pl.pallas_call(functools.partial(strip_kernel, rows, far), out_shape=[jax...]
  transfers between devices with their start and end apart: 12 -> 12, of which waited for: 5 -> 5; matrix products, arithmetic and copies ran while one was open for 1% -> 1% of each run, Pallas kernels for 6% -> 9%
where the time goes in v3:
time: 31 us; the launch traced here: 30.9 us
  starting transfers between devices  16.4 us (53%)
  waiting for transfers between devices  10.6 us (34%)
  Pallas kernels  2.77 us (9%)
  other arithmetic  0.89 us (3%)
    ppermute x11, starting transfers between devices, swap(): return lax.ppermute(array, 'mem', [(i, i ^ bits) for i in range(16)])  13.9 us
    ppermute x11, waiting for transfers between devices, swap(): return lax.ppermute(array, 'mem', [(i, i ^ bits) for i in range(16)])  10.6 us
    ppermute x1, starting transfers between devices, edges(): return lax.ppermute(array, 'mem', pairs)  2.57 us
    pallas_call x2, Pallas kernels, one_strip(): pl.pallas_call(functools.partial(strip_kernel, rows, far), out_shape=[jax...  1.42 us
    pallas_call x1, Pallas kernels, windows(): pl.pallas_call(functools.partial(window_kernel, strip, wanted), out_shape...  1.35 us
    reshape x1, other arithmetic, by_halves(): (total * (1.0 / (members - 1))).astype(jnp.bfloat16).reshape(gradient.shape)  0.65 us
  transfers between devices with their start and end apart: 12, of which 5 were waited for; matrix products, arithmetic and copies ran while one was open for 1% of the time, Pallas kernels for 9%

profile of v3, /device:TPU:0, one launch (start us, length us, event | category | flops | bytes accessed | tf_op | source)
XLA Modules:
  0.0 30.9 jit_solution(12983855045797891179)
XLA Ops:
  0.0 4.1 %collective-permute-start.3 = (bf16[16,4,256]{2,1,0:T(4,128)(2,1)}, bf16[16,4,256]{2,1,0:T(4,128)(2,1)S(1)}, u32[]{:S(2)}, u32[]{:S(2)}) collective-permute-start(bf16[16,4,256]{2,1,0:T(4,128)(2,1)} %bitcast.16), channel_id=1, source_target_pairs={{0,8},{1,9},{2,10},{3,11},{4,12},{5,13},{6,14},{7,15},{8,0},{9,1},... | collective-permute-start | bytes 98312 | tf_op jit(solution)/shard_map/ppermute | solution.py:61
  4.1 1.4 %shard_map.28 = (bf16[48,4,256]{2,1,0:T(4,128)(2,1)S(1)}, bf16[48,4,256]{2,1,0:T(4,128)(2,1)S(1)}, bf16[48,4,256]{2,1,0:T(4,128)(2,1)S(1)}, bf16[48,4,256]{2,1,0...) custom-call(s32[1]{0:T(128)} %bitcast.me_ref, ...), custom_call_target="tpu_custom_call" | custom-call | tf_op jit(solution)/shard_map/pallas_call | solution.py:108
  5.4 1.1 %collective-permute-done.3.block_ref = bf16[16,4,256]{2,1,0:T(4,128)(2,1)S(1)} collective-permute-done((bf16[16,4,256]{2,1,0:T(4,128)(2,1)}, bf16[16,4,256]{2,1,0:T(4,128)(2,1)S(1)}, u32[]{:S(2)}, u32[]{:S(2)}) %collective-permute-start.3) | collective-permute-done | bytes 32800 | tf_op jit(solution)/shard_map/ppermute | solution.py:61
  6.6 2.6 %collective-permute-start.4 = (bf16[2,8,4,256]{3,2,1,0:T(4,128)(2,1)S(1)}, bf16[2,8,4,256]{3,2,1,0:T(4,128)(2,1)S(1)}, u32[]{:S(2)}, u32[]{:S(2)}) collective-permute-start(bf16[2,8,4,256]{3,2,1,0:T(4,128)(2,1)S(1)} %fusion.2), channel_id=1, source_target_pairs={{0,6},{1,3},{2,0},{3,5},{4,2},{5,7},{6,4},{7,1},{8,14},{9,11},{10,... | collective-permute-start | bytes 98312 | tf_op jit(solution)/shard_map/ppermute | solution.py:72
  9.1 0.5 %collective-permute-start = (bf16[48,4,256]{2,1,0:T(4,128)(2,1)S(1)}, bf16[48,4,256]{2,1,0:T(4,128)(2,1)S(1)}, u32[]{:S(2)}, u32[]{:S(2)}) collective-permute-start(bf16[48,4,256]{2,1,0:T(4,128)(2,1)S(1)} %get-tuple-element.18), channel_id=1, source_target_pairs={{0,6},{1,7},{2,4},{3,5},{4,2},{5,3},{6,0},{7,1},{8,14},{9,15},{10,... | collective-permute-start | bytes 294920 | tf_op jit(solution)/shard_map/ppermute | solution.py:61
  9.6 1.6 %collective-permute-start.1 = (bf16[48,4,256]{2,1,0:T(4,128)(2,1)S(1)}, bf16[48,4,256]{2,1,0:T(4,128)(2,1)S(1)}, u32[]{:S(2)}, u32[]{:S(2)}) collective-permute-start(bf16[48,4,256]{2,1,0:T(4,128)(2,1)S(1)} %get-tuple-element.19), channel_id=1, source_target_pairs={{0,2},{1,3},{2,0},{3,1},{4,6},{5,7},{6,4},{7,5},{8,10},{9,11},{10,... | collective-permute-start | bytes 294920 | tf_op jit(solution)/shard_map/ppermute | solution.py:61
  11.3 1.3 %collective-permute-start.2 = (bf16[48,4,256]{2,1,0:T(4,128)(2,1)S(1)}, bf16[48,4,256]{2,1,0:T(4,128)(2,1)S(1)}, u32[]{:S(2)}, u32[]{:S(2)}) collective-permute-start(bf16[48,4,256]{2,1,0:T(4,128)(2,1)S(1)} %get-tuple-element.20), channel_id=1, source_target_pairs={{0,4},{1,5},{2,6},{3,7},{4,0},{5,1},{6,2},{7,3},{8,12},{9,13},{10,... | collective-permute-start | bytes 294920 | tf_op jit(solution)/shard_map/ppermute | solution.py:61
  12.6 0.5 %collective-permute-start.7 = (bf16[48,4,256]{2,1,0:T(4,128)(2,1)S(1)}, bf16[48,4,256]{2,1,0:T(4,128)(2,1)S(1)}, u32[]{:S(2)}, u32[]{:S(2)}) collective-permute-start(bf16[48,4,256]{2,1,0:T(4,128)(2,1)S(1)} %get-tuple-element.24), channel_id=1, source_target_pairs={{0,6},{1,7},{2,4},{3,5},{4,2},{5,3},{6,0},{7,1},{8,14},{9,15},{10,... | collective-permute-start | bytes 294920 | tf_op jit(solution)/shard_map/ppermute | solution.py:61
  13.1 1.6 %collective-permute-start.8 = (bf16[48,4,256]{2,1,0:T(4,128)(2,1)S(1)}, bf16[48,4,256]{2,1,0:T(4,128)(2,1)S(1)}, u32[]{:S(2)}, u32[]{:S(2)}) collective-permute-start(bf16[48,4,256]{2,1,0:T(4,128)(2,1)S(1)} %get-tuple-element.25), channel_id=1, source_target_pairs={{0,2},{1,3},{2,0},{3,1},{4,6},{5,7},{6,4},{7,5},{8,10},{9,11},{10,... | collective-permute-start | bytes 294920 | tf_op jit(solution)/shard_map/ppermute | solution.py:61
  14.8 0.1 pad_maximum_fusion
  14.9 3.4 %collective-permute-done.7.b_ref = bf16[48,4,256]{2,1,0:T(4,128)(2,1)S(1)} collective-permute-done((bf16[48,4,256]{2,1,0:T(4,128)(2,1)S(1)}, bf16[48,4,256]{2,1,0:T(4,128)(2,1)S(1)}, u32[]{:S(2)}, u32[]{:S(2)}) %collective-permute-start.7) | collective-permute-done | bytes 98336 | tf_op jit(solution)/shard_map/ppermute | solution.py:61
  18.2 0.7 %collective-permute-start.9 = (bf16[48,4,256]{2,1,0:T(4,128)(2,1)S(1)}, bf16[48,4,256]{2,1,0:T(4,128)(2,1)S(1)}, u32[]{:S(2)}, u32[]{:S(2)}) collective-permute-start(bf16[48,4,256]{2,1,0:T(4,128)(2,1)S(1)} %get-tuple-element.26), channel_id=1, source_target_pairs={{0,4},{1,5},{2,6},{3,7},{4,0},{5,1},{6,2},{7,3},{8,12},{9,13},{10,... | collective-permute-start | bytes 294920 | tf_op jit(solution)/shard_map/ppermute | solution.py:61
  18.9 0.1 collective-permute-done.8.c_ref
  19.0 0.0 collective-permute-start.5
  19.0 0.1 select_convert_fusion.band_ref
  19.1 3.8 %collective-permute-done.9.d_ref = bf16[48,4,256]{2,1,0:T(4,128)(2,1)S(1)} collective-permute-done((bf16[48,4,256]{2,1,0:T(4,128)(2,1)S(1)}, bf16[48,4,256]{2,1,0:T(4,128)(2,1)S(1)}, u32[]{:S(2)}, u32[]{:S(2)}) %collective-permute-start.9) | collective-permute-done | bytes 98336 | tf_op jit(solution)/shard_map/ppermute | solution.py:61
  22.9 0.7 %far.1 = (f32[16,4,256]{2,1,0:T(4,128)S(1)}, bf16[16,4,256]{2,1,0:T(4,128)(2,1)S(1)}) custom-call(s32[1]{0:T(128)} %bitcast.me_ref, bf16[2,48,4,256]{3,2,1,0:T(4,128)(2,1)S(1)} %get-tuple-element.17.a_ref, bf16[48,4,256]{2,1,0:T(4,128)(2,1)S(1)} %collective-permute-done.7.b_ref, bf16[48,4,256]{2,1,0:T(4,128)(2,1)S(1)} %collective-permute-done.8.c_ref, ...), custom_call_target="tpu_custom_call" | custom-call | tf_op jit(solution)/shard_map/far/pallas_call | solution.py:186
  23.6 0.1 collective-permute-start.10
  23.7 0.0 collective-permute-done.b_ref
  23.7 0.7 %near.1 = (f32[16,4,256]{2,1,0:T(4,128)S(1)}, bf16[16,4,256]{2,1,0:T(4,128)(2,1)S(1)}) custom-call(s32[1]{0:T(128)} %bitcast.me_ref, bf16[2,48,4,256]{3,2,1,0:T(4,128)(2,1)S(1)} %get-tuple-element.17.a_ref, bf16[48,4,256]{2,1,0:T(4,128)(2,1)S(1)} %collective-permute-done.b_ref, bf16[48,4,256]{2,1,0:T(4,128)(2,1)S(1)} %collective-permute-done.1.c_ref, ...), custom_call_target="tpu_custom_call" | custom-call | tf_op jit(solution)/shard_map/near/pallas_call | solution.py:186
  24.4 0.5 %collective-permute-start.6 = (bf16[16,4,256]{2,1,0:T(4,128)(2,1)S(1)}, bf16[16,4,256]{2,1,0:T(4,128)(2,1)S(1)}, u32[]{:S(2)}, u32[]{:S(2)}) collective-permute-start(bf16[16,4,256]{2,1,0:T(4,128)(2,1)S(1)} %get-tuple-element.23), channel_id=1, source_target_pairs={{0,1},{1,0},{2,3},{3,2},{4,5},{5,4},{6,7},{7,6},{8,9},{9,8},{10,11... | collective-permute-start | bytes 98312 | tf_op jit(solution)/shard_map/ppermute | solution.py:61
  25.0 2.9 %collective-permute-start.11 = (bf16[16,4,256]{2,1,0:T(4,128)(2,1)S(1)}, bf16[16,4,256]{2,1,0:T(4,128)(2,1)S(1)}, u32[]{:S(2)}, u32[]{:S(2)}) collective-permute-start(bf16[16,4,256]{2,1,0:T(4,128)(2,1)S(1)} %add_convert_fusion), channel_id=1, source_target_pairs={{0,8},{1,9},{2,10},{3,11},{4,12},{5,13},{6,14},{7,15},{8,0},{9,1},... | collective-permute-start | bytes 98312 | tf_op jit(solution)/shard_map/ppermute | solution.py:61
  27.9 2.3 %collective-permute-done.11 = bf16[16,4,256]{2,1,0:T(4,128)(2,1)S(1)} collective-permute-done((bf16[16,4,256]{2,1,0:T(4,128)(2,1)S(1)}, bf16[16,4,256]{2,1,0:T(4,128)(2,1)S(1)}, u32[]{:S(2)}, u32[]{:S(2)}) %collective-permute-start.11) | collective-permute-done | bytes 32800 | tf_op jit(solution)/shard_map/ppermute | solution.py:61
  30.2 0.6 %fusion = bf16[16,4,1,256]{3,1,2,0:T(4,128)(2,1)} fusion(bf16[16,4,256]{2,1,0:T(4,128)(2,1)S(1)} %collective-permute-done.11, f32[16,4,256]{2,1,0:T(4,128)S(1)} %get-tuple-element.22, bf16[16,4,256]{2,1,0:T(4,128)(2,1)S(1)} %collective-permute-done.6), kind=kLoop, calls=%fused_computation.7 | loop fusion | flops 98304 | bytes 163840 | tf_op jit(solution)/shard_map/reshape | solution.py:255
  (9 shorter events, 0.1 us)
Async XLA Ops:
  0.0 6.5 %collective-permute-start.3 = (bf16[16,4,256]{2,1,0:T(4,128)(2,1)}, bf16[16,4,256]{2,1,0:T(4,128)(2,1)S(1)}, u32[]{:S(2)}, u32[]{:S(2)}) collective-permute-start(bf16[16,4,256]{2,1,0:T(4,128)(2,1)} %bitcast.16), channel_id=1, source_target_pairs={{0,8},{1,9},{2,10},{3,11},{4,12},{5,13},{6,14},{7,15},{8,0},{9,1},... | collective-permute-start | bytes 98312 | tf_op jit(solution)/shard_map/ppermute | solution.py:61
  6.6 6.6 %collective-permute-start.4 = (bf16[2,8,4,256]{3,2,1,0:T(4,128)(2,1)S(1)}, bf16[2,8,4,256]{3,2,1,0:T(4,128)(2,1)S(1)}, u32[]{:S(2)}, u32[]{:S(2)}) collective-permute-start(bf16[2,8,4,256]{3,2,1,0:T(4,128)(2,1)S(1)} %fusion.2), channel_id=1, source_target_pairs={{0,6},{1,3},{2,0},{3,5},{4,2},{5,7},{6,4},{7,1},{8,14},{9,11},{10,... | collective-permute-start | bytes 98312 | tf_op jit(solution)/shard_map/ppermute | solution.py:72
  9.1 14.5 %collective-permute-start = (bf16[48,4,256]{2,1,0:T(4,128)(2,1)S(1)}, bf16[48,4,256]{2,1,0:T(4,128)(2,1)S(1)}, u32[]{:S(2)}, u32[]{:S(2)}) collective-permute-start(bf16[48,4,256]{2,1,0:T(4,128)(2,1)S(1)} %get-tuple-element.18), channel_id=1, source_target_pairs={{0,6},{1,7},{2,4},{3,5},{4,2},{5,3},{6,0},{7,1},{8,14},{9,15},{10,... | collective-permute-start | bytes 294920 | tf_op jit(solution)/shard_map/ppermute | solution.py:61
  9.6 14.0 %collective-permute-start.1 = (bf16[48,4,256]{2,1,0:T(4,128)(2,1)S(1)}, bf16[48,4,256]{2,1,0:T(4,128)(2,1)S(1)}, u32[]{:S(2)}, u32[]{:S(2)}) collective-permute-start(bf16[48,4,256]{2,1,0:T(4,128)(2,1)S(1)} %get-tuple-element.19), channel_id=1, source_target_pairs={{0,2},{1,3},{2,0},{3,1},{4,6},{5,7},{6,4},{7,5},{8,10},{9,11},{10,... | collective-permute-start | bytes 294920 | tf_op jit(solution)/shard_map/ppermute | solution.py:61
  11.3 12.4 %collective-permute-start.2 = (bf16[48,4,256]{2,1,0:T(4,128)(2,1)S(1)}, bf16[48,4,256]{2,1,0:T(4,128)(2,1)S(1)}, u32[]{:S(2)}, u32[]{:S(2)}) collective-permute-start(bf16[48,4,256]{2,1,0:T(4,128)(2,1)S(1)} %get-tuple-element.20), channel_id=1, source_target_pairs={{0,4},{1,5},{2,6},{3,7},{4,0},{5,1},{6,2},{7,3},{8,12},{9,13},{10,... | collective-permute-start | bytes 294920 | tf_op jit(solution)/shard_map/ppermute | solution.py:61
  12.6 5.6 %collective-permute-start.7 = (bf16[48,4,256]{2,1,0:T(4,128)(2,1)S(1)}, bf16[48,4,256]{2,1,0:T(4,128)(2,1)S(1)}, u32[]{:S(2)}, u32[]{:S(2)}) collective-permute-start(bf16[48,4,256]{2,1,0:T(4,128)(2,1)S(1)} %get-tuple-element.24), channel_id=1, source_target_pairs={{0,6},{1,7},{2,4},{3,5},{4,2},{5,3},{6,0},{7,1},{8,14},{9,15},{10,... | collective-permute-start | bytes 294920 | tf_op jit(solution)/shard_map/ppermute | solution.py:61
  13.1 5.9 %collective-permute-start.8 = (bf16[48,4,256]{2,1,0:T(4,128)(2,1)S(1)}, bf16[48,4,256]{2,1,0:T(4,128)(2,1)S(1)}, u32[]{:S(2)}, u32[]{:S(2)}) collective-permute-start(bf16[48,4,256]{2,1,0:T(4,128)(2,1)S(1)} %get-tuple-element.25), channel_id=1, source_target_pairs={{0,2},{1,3},{2,0},{3,1},{4,6},{5,7},{6,4},{7,5},{8,10},{9,11},{10,... | collective-permute-start | bytes 294920 | tf_op jit(solution)/shard_map/ppermute | solution.py:61
  18.2 4.6 %collective-permute-start.9 = (bf16[48,4,256]{2,1,0:T(4,128)(2,1)S(1)}, bf16[48,4,256]{2,1,0:T(4,128)(2,1)S(1)}, u32[]{:S(2)}, u32[]{:S(2)}) collective-permute-start(bf16[48,4,256]{2,1,0:T(4,128)(2,1)S(1)} %get-tuple-element.26), channel_id=1, source_target_pairs={{0,4},{1,5},{2,6},{3,7},{4,0},{5,1},{6,2},{7,3},{8,12},{9,13},{10,... | collective-permute-start | bytes 294920 | tf_op jit(solution)/shard_map/ppermute | solution.py:61
  19.0 3.9 %collective-permute-start.5 = (bf16[48,4,256]{2,1,0:T(4,128)(2,1)S(1)}, bf16[48,4,256]{2,1,0:T(4,128)(2,1)S(1)}, u32[]{:S(2)}, u32[]{:S(2)}) collective-permute-start(bf16[48,4,256]{2,1,0:T(4,128)(2,1)S(1)} %pad_maximum_fusion), channel_id=1, source_target_pairs={{0,1},{1,0},{2,3},{3,2},{4,5},{5,4},{6,7},{7,6},{8,9},{9,8},{10,11... | collective-permute-start | bytes 294920 | tf_op jit(solution)/shard_map/ppermute | solution.py:61
  23.6 1.4 %collective-permute-start.10 = (bf16[16,4,256]{2,1,0:T(4,128)(2,1)S(1)}, bf16[16,4,256]{2,1,0:T(4,128)(2,1)S(1)}, u32[]{:S(2)}, u32[]{:S(2)}) collective-permute-start(bf16[16,4,256]{2,1,0:T(4,128)(2,1)S(1)} %get-tuple-element.28), channel_id=1, source_target_pairs={{0,1},{1,0},{2,3},{3,2},{4,5},{5,4},{6,7},{7,6},{8,9},{9,8},{10,11... | collective-permute-start | bytes 98312 | tf_op jit(solution)/shard_map/ppermute | solution.py:61
  24.4 3.5 %collective-permute-start.6 = (bf16[16,4,256]{2,1,0:T(4,128)(2,1)S(1)}, bf16[16,4,256]{2,1,0:T(4,128)(2,1)S(1)}, u32[]{:S(2)}, u32[]{:S(2)}) collective-permute-start(bf16[16,4,256]{2,1,0:T(4,128)(2,1)S(1)} %get-tuple-element.23), channel_id=1, source_target_pairs={{0,1},{1,0},{2,3},{3,2},{4,5},{5,4},{6,7},{7,6},{8,9},{9,8},{10,11... | collective-permute-start | bytes 98312 | tf_op jit(solution)/shard_map/ppermute | solution.py:61
  25.0 5.2 %collective-permute-start.11 = (bf16[16,4,256]{2,1,0:T(4,128)(2,1)S(1)}, bf16[16,4,256]{2,1,0:T(4,128)(2,1)S(1)}, u32[]{:S(2)}, u32[]{:S(2)}) collective-permute-start(bf16[16,4,256]{2,1,0:T(4,128)(2,1)S(1)} %add_convert_fusion), channel_id=1, source_target_pairs={{0,8},{1,9},{2,10},{3,11},{4,12},{5,13},{6,14},{7,15},{8,0},{9,1},... | collective-permute-start | bytes 98312 | tf_op jit(solution)/shard_map/ppermute | solution.py:61
